TPU v7x, 1024 devices: a whole 8x8x8 slice. The times are simulated.
1024 devices in a mesh: seq: 32 (over y_lo, z), chan: 32 (over x, y_hi, core).
Axes of the slice: x: 8, y: 8 (y_hi: 2, y_lo: 4; y = y_hi * 4 + y_lo), z: 8, core: 2. Of those that a mesh axis runs over, the one named last changes fastest.
Arguments:
- query_proj: bfloat16 [4096, 8192], P('seq', 'chan'), may hold values from -18 to 18
- key_proj: bfloat16 [4096, 8192], P('seq', 'chan'), may hold values from -6 to 6
- value_proj: bfloat16 [4096, 8192], P('seq', 'chan'), may hold values from -6 to 6
- filters: bfloat16 [8192, 4096], P('chan', 'seq'), may hold values from -48 to 48
- norm_gain: float32 [8192], P('chan'), may hold values from 0.25 to 1.75
- out_grad: bfloat16 [4096, 8192], P('seq', 'chan'), may hold values from -6 to 6
Outputs:
- normed: bfloat16 [4096, 8192], P('seq', 'chan')
- query_grad: bfloat16 [4096, 8192], P('seq', 'chan')
- key_grad: bfloat16 [4096, 8192], P('seq', 'chan')
- value_grad: bfloat16 [4096, 8192], P('seq', 'chan')
All inputs are finite; a program needn't handle non-finite values.
Results may differ from a plain program's by a relative error of at most 0.0095.
Values may be sent and summed in bfloat16 or wider, within the bound.
No kernel may reach another device: no remote copies, remote signals or barrier semaphores. Data moves between devices by JAX's collectives and lax.ppermute only.
A program may use at most 32 MiB of HBM per device.

v0:
```python
import math

import jax
import jax.numpy as jnp
from jax import lax
from jax.sharding import PartitionSpec as P

D = 8192


EPSILON = 1e-05
HIGHEST = lax.Precision.HIGHEST


def rounded(array):
    return lax.optimization_barrier(array.astype(jnp.bfloat16)).astype(jnp.float32)


def split_size(extent):
    factor = 1
    while factor * factor < extent and extent % (2 * factor) == 0:
        factor = factor * 2
    return factor


def phase_table(row_count, col_count, extent):
    phases = (
        jnp.arange(row_count, dtype=jnp.int32)[:, None]
        * jnp.arange(col_count, dtype=jnp.int32)[None, :]
        % extent
    )
    angles = phases.astype(jnp.float32) * (-2.0 * math.pi / extent)
    return (jnp.cos(angles), jnp.sin(angles))


def make_tables(extent):
    outer_size = split_size(extent)
    inner_size = extent // outer_size
    outer_dft = phase_table(outer_size, outer_size, outer_size)
    twiddle = phase_table(outer_size, inner_size, extent)
    inner_dft = phase_table(inner_size, inner_size, inner_size)
    return (outer_dft, twiddle, inner_dft)


def forward_real(signal, tables):
    outer_dft, twiddle, inner_dft = tables
    batch_size = signal.shape[0]
    outer_size = outer_dft[0].shape[0]
    inner_size = inner_dft[0].shape[0]
    half_rows = outer_size // 2
    folded = signal.reshape(batch_size, half_rows, inner_size)
    partial_re = jnp.einsum("kn,bnm->bkm", outer_dft[0][:, :half_rows], folded, precision=HIGHEST)
    partial_im = jnp.einsum("kn,bnm->bkm", outer_dft[1][:, :half_rows], folded, precision=HIGHEST)
    turned_re = partial_re * twiddle[0] - partial_im * twiddle[1]
    turned_im = partial_re * twiddle[1] + partial_im * twiddle[0]
    spec_re = jnp.einsum("bkn,jn->bkj", turned_re, inner_dft[0], precision=HIGHEST) - jnp.einsum(
        "bkn,jn->bkj", turned_im, inner_dft[1], precision=HIGHEST
    )
    spec_im = jnp.einsum("bkn,jn->bkj", turned_re, inner_dft[1], precision=HIGHEST) + jnp.einsum(
        "bkn,jn->bkj", turned_im, inner_dft[0], precision=HIGHEST
    )
    return (spec_re, spec_im)


def inverse_real(spec_re, spec_im, tables):
    outer_dft, twiddle, inner_dft = tables
    batch_size = spec_re.shape[0]
    outer_size = outer_dft[0].shape[0]
    extent = outer_size * inner_dft[0].shape[0]
    half_rows = outer_size // 2
    back_re = jnp.einsum("bkj,jn->bkn", spec_re, inner_dft[0], precision=HIGHEST) + jnp.einsum(
        "bkj,jn->bkn", spec_im, inner_dft[1], precision=HIGHEST
    )
    back_im = jnp.einsum("bkj,jn->bkn", spec_im, inner_dft[0], precision=HIGHEST) - jnp.einsum(
        "bkj,jn->bkn", spec_re, inner_dft[1], precision=HIGHEST
    )
    turned_re = back_re * twiddle[0] + back_im * twiddle[1]
    turned_im = back_im * twiddle[0] - back_re * twiddle[1]
    signal = jnp.einsum(
        "nk,bkm->bnm", outer_dft[0][:half_rows], turned_re, precision=HIGHEST
    ) + jnp.einsum("nk,bkm->bnm", outer_dft[1][:half_rows], turned_im, precision=HIGHEST)
    return signal.reshape(batch_size, -1) * (1.0 / extent)


def convolve_own(source, filter_own, tables):
    source_re, source_im = forward_real(source, tables)
    kernel_re, kernel_im = forward_real(filter_own.astype(jnp.float32), tables)
    convolved = inverse_real(
        source_re * kernel_re - source_im * kernel_im,
        source_re * kernel_im + source_im * kernel_re,
        tables,
    )
    return (convolved.astype(jnp.bfloat16), (kernel_re, kernel_im))


def correlate_own(weighted, kernel, tables):
    weight_re, weight_im = forward_real(weighted, tables)
    kernel_re, kernel_im = kernel
    cross_re = weight_re * kernel_re + weight_im * kernel_im
    cross_im = weight_im * kernel_re - weight_re * kernel_im
    return inverse_real(cross_re, cross_im, tables).astype(jnp.bfloat16)


def owner_forward(query_own, key_own, value_own, filter_own, tables):
    source = rounded(key_own.astype(jnp.float32) * value_own.astype(jnp.float32))
    convolved, kernel = convolve_own(source, filter_own, tables)
    product = (query_own.astype(jnp.float32) * convolved.astype(jnp.float32)).astype(jnp.bfloat16)
    return (product, convolved, kernel)


def owner_backward(grad_own, query_own, key_own, value_own, convolved, kernel, tables):
    grad_wide = grad_own.astype(jnp.float32)
    query_grad = (grad_wide * convolved.astype(jnp.float32)).astype(jnp.bfloat16)
    weighted = rounded(grad_wide * query_own.astype(jnp.float32))
    spread = lax.optimization_barrier(correlate_own(weighted, kernel, tables)).astype(jnp.float32)
    key_grad = (spread * value_own.astype(jnp.float32)).astype(jnp.bfloat16)
    value_grad = (spread * key_own.astype(jnp.float32)).astype(jnp.bfloat16)
    return (query_grad, key_grad, value_grad)


def per_device(query_proj, key_proj, value_proj, filters, norm_gain, out_grad):
    seq_count = lax.axis_size("seq")
    seq_length = query_proj.shape[0] * seq_count
    tables = make_tables(2 * seq_length)
    query_own, key_own, value_own, filter_own = (
        lax.all_to_all(query_proj.T, "seq", split_axis=0, concat_axis=1, tiled=True),
        lax.all_to_all(key_proj.T, "seq", split_axis=0, concat_axis=1, tiled=True),
        lax.all_to_all(value_proj.T, "seq", split_axis=0, concat_axis=1, tiled=True),
        lax.all_to_all(filters, "seq", split_axis=0, concat_axis=1, tiled=True),
    )
    product, convolved, kernel = owner_forward(query_own, key_own, value_own, filter_own, tables)
    prod_wide = lax.all_to_all(product, "seq", split_axis=1, concat_axis=0, tiled=True).T.astype(
        jnp.float32
    )
    gained = out_grad.astype(jnp.float32) * norm_gain[None, :]
    square_sum, cross_sum = lax.psum(
        (jnp.sum(prod_wide * prod_wide, axis=1), jnp.sum(gained * prod_wide, axis=1)), "chan"
    )
    scale = lax.rsqrt(square_sum / D + EPSILON)[:, None]
    normed = (prod_wide * scale * norm_gain[None, :]).astype(jnp.bfloat16)
    grad_tokens = (
        gained * scale - prod_wide * (cross_sum[:, None] * scale * scale * scale / D)
    ).astype(jnp.bfloat16)
    grad_own = lax.all_to_all(grad_tokens.T, "seq", split_axis=0, concat_axis=1, tiled=True)
    grads_own = owner_backward(grad_own, query_own, key_own, value_own, convolved, kernel, tables)
    query_grad, key_grad, value_grad = (
        lax.all_to_all(grads_own[0], "seq", split_axis=1, concat_axis=0, tiled=True),
        lax.all_to_all(grads_own[1], "seq", split_axis=1, concat_axis=0, tiled=True),
        lax.all_to_all(grads_own[2], "seq", split_axis=1, concat_axis=0, tiled=True),
    )
    return (normed, query_grad.T, key_grad.T, value_grad.T)


def solution(mesh):
    placed = (
        P("seq", "chan"),
        P("seq", "chan"),
        P("seq", "chan"),
        P("chan", "seq"),
        P("chan"),
        P("seq", "chan"),
    )
    return jax.shard_map(
        per_device,
        mesh=mesh,
        in_specs=placed,
        out_specs=(P("seq", "chan"), P("seq", "chan"), P("seq", "chan"), P("seq", "chan")),
        check_vma=False,
    )
```

profile of v0, /device:TPU:1, one launch (start us, length us, event | category | flops | bytes accessed | tf_op | source)
XLA Modules:
  0.0 238.3 jit_solution(6977607015802773746)
XLA Ops:
  0.6 1.6 copy.64
  2.2 21.1 %all-to-all-start.1 = ((bf16[32,8,128]{2,1,0:T(8,128)(2,1)}), bf16[32,8,128]{2,1,0:T(8,128)(2,1)S(1)}, u32[]{:S(2)}, u32[]{:S(2)}) async-start(bf16[32,8,128]{2,1,0:T(8,128)(2,1)} %bitcast.4), calls=%async_computation.1 | async-start | bytes 131072 | tf_op jit(solution)/shard_map/all_to_all | solution.py:127
  23.3 0.7 copy.65
  24.2 8.3 %all-to-all-done.1 = bf16[32,8,128]{2,1,0:T(8,128)(2,1)S(1)} async-done(((bf16[32,8,128]{2,1,0:T(8,128)(2,1)}), bf16[32,8,128]{2,1,0:T(8,128)(2,1)S(1)}, u32[]{:S(2)}, u32[]{:S(2)}) %all-to-all-start.1) | async-done | bytes 65568 | tf_op jit(solution)/shard_map/all_to_all | solution.py:127
  32.5 3.9 %all-to-all-start.2 = ((bf16[32,8,128]{2,1,0:T(8,128)(2,1)}), bf16[32,8,128]{2,1,0:T(8,128)(2,1)S(1)}, u32[]{:S(2)}, u32[]{:S(2)}) async-start(bf16[32,8,128]{2,1,0:T(8,128)(2,1)} %bitcast.8), calls=%async_computation.2 | async-start | bytes 131072 | tf_op jit(solution)/shard_map/all_to_all | solution.py:128
  37.2 0.7 copy.63
  38.2 7.3 %all-to-all-done.2 = bf16[32,8,128]{2,1,0:T(8,128)(2,1)S(1)} async-done(((bf16[32,8,128]{2,1,0:T(8,128)(2,1)}), bf16[32,8,128]{2,1,0:T(8,128)(2,1)S(1)}, u32[]{:S(2)}, u32[]{:S(2)}) %all-to-all-start.2) | async-done | bytes 65568 | tf_op jit(solution)/shard_map/all_to_all | solution.py:128
  45.5 3.9 %all-to-all-start.3 = ((bf16[32,8,128]{2,1,0:T(8,128)(2,1)}), bf16[32,8,128]{2,1,0:T(8,128)(2,1)S(1)}, u32[]{:S(2)}, u32[]{:S(2)}) async-start(bf16[32,8,128]{2,1,0:T(8,128)(2,1)} %bitcast.17), calls=%async_computation.3 | async-start | bytes 131072 | tf_op jit(solution)/shard_map/all_to_all | solution.py:129
  50.2 8.3 %all-to-all-done.3 = bf16[32,8,128]{2,1,0:T(8,128)(2,1)S(1)} async-done(((bf16[32,8,128]{2,1,0:T(8,128)(2,1)}), bf16[32,8,128]{2,1,0:T(8,128)(2,1)S(1)}, u32[]{:S(2)}, u32[]{:S(2)}) %all-to-all-start.3) | async-done | bytes 65568 | tf_op jit(solution)/shard_map/all_to_all | solution.py:129
  58.5 3.9 %all-to-all-start = ((bf16[32,8,128]{2,1,0:T(8,128)(2,1)}), bf16[32,8,128]{2,1,0:T(8,128)(2,1)S(1)}, u32[]{:S(2)}, u32[]{:S(2)}) async-start(bf16[32,8,128]{2,1,0:T(8,128)(2,1)} %bitcast.1), calls=%async_computation | async-start | bytes 131072 | tf_op jit(solution)/shard_map/all_to_all | solution.py:126
  70.8 0.7 all-to-all-done
  72.3 9.0 %all-to-all-start.4 = ((bf16[8,32,128]{2,0,1:T(8,128)(2,1)}), bf16[8,32,128]{2,0,1:T(8,128)(2,1)S(1)}, u32[]{:S(2)}, u32[]{:S(2)}) async-start(bf16[8,32,128]{2,0,1:T(8,128)(2,1)} %fusion.30), calls=%async_computation.4 | async-start | bytes 131072 | tf_op jit(solution)/shard_map/all_to_all | solution.py:132
  81.4 9.0 %all-to-all-done.4 = bf16[8,32,128]{2,0,1:T(8,128)(2,1)S(1)} async-done(((bf16[8,32,128]{2,0,1:T(8,128)(2,1)}), bf16[8,32,128]{2,0,1:T(8,128)(2,1)S(1)}, u32[]{:S(2)}, u32[]{:S(2)}) %all-to-all-start.4) | async-done | bytes 65568 | tf_op jit(solution)/shard_map/all_to_all | solution.py:132
  90.5 89.7 %all-reduce = (f32[128]{0:T(128)S(1)}, f32[128]{0:T(128)S(1)}) all-reduce(f32[128]{0:T(128)S(1)} %get-tuple-element.13, f32[128]{0:T(128)S(1)} %get-tuple-element.12), channel_id=1, replica_groups=mesh['seq'=32,'chan'=32] {'chan'}, use_global_device_ids=true, to_apply=%region_1.2 | all-reduce | flops 256 | bytes 2048 | tf_op jit(solution)/shard_map/psum | solution.py:136
  180.4 12.1 %all_to_all.132 = bf16[32,8,128]{2,1,0:T(8,128)(2,1)S(1)} all-to-all(bf16[32,8,128]{2,1,0:T(8,128)(2,1)S(1)} %get-tuple-element.20), channel_id=1, replica_groups=mesh['seq'=32,'chan'=32] {'seq'}, dimensions={0} | all-to-all | bytes 131072 | tf_op jit(solution)/shard_map/all_to_all | solution.py:144
  199.5 12.1 %all_to_all.133 = bf16[8,32,128]{2,0,1:T(8,128)(2,1)S(1)} all-to-all(bf16[8,32,128]{2,0,1:T(8,128)(2,1)S(1)} %get-tuple-element.23), channel_id=1, replica_groups=mesh['seq'=32,'chan'=32] {'seq'}, dimensions={1} | all-to-all | bytes 131072 | tf_op jit(solution)/shard_map/all_to_all | solution.py:148
  211.6 3.9 %all-to-all-start.8 = ((bf16[8,32,128]{2,0,1:T(8,128)(2,1)}), bf16[8,32,128]{2,0,1:T(8,128)(2,1)S(1)}, u32[]{:S(2)}, u32[]{:S(2)}) async-start(bf16[8,32,128]{2,0,1:T(8,128)(2,1)} %get-tuple-element.22), calls=%async_computation.8 | async-start | bytes 131072 | tf_op jit(solution)/shard_map/all_to_all | solution.py:149
  216.2 8.4 %all-to-all-done.8 = bf16[8,32,128]{2,0,1:T(8,128)(2,1)S(1)} async-done(((bf16[8,32,128]{2,0,1:T(8,128)(2,1)}), bf16[8,32,128]{2,0,1:T(8,128)(2,1)S(1)}, u32[]{:S(2)}, u32[]{:S(2)}) %all-to-all-start.8) | async-done | bytes 65568 | tf_op jit(solution)/shard_map/all_to_all | solution.py:149
  224.6 3.9 %all-to-all-start.6 = ((bf16[8,32,128]{2,0,1:T(8,128)(2,1)}), bf16[8,32,128]{2,0,1:T(8,128)(2,1)S(1)}, u32[]{:S(2)}, u32[]{:S(2)}) async-start(bf16[8,32,128]{2,0,1:T(8,128)(2,1)} %fusion.32), calls=%async_computation.6 | async-start | bytes 131072 | tf_op jit(solution)/shard_map/all_to_all | solution.py:147
  228.5 0.7 copy.96
  229.2 0.7 copy.98
  229.9 0.7 copy.99
  230.7 6.9 %all-to-all-done.6 = bf16[8,32,128]{2,0,1:T(8,128)(2,1)S(1)} async-done(((bf16[8,32,128]{2,0,1:T(8,128)(2,1)}), bf16[8,32,128]{2,0,1:T(8,128)(2,1)S(1)}, u32[]{:S(2)}, u32[]{:S(2)}) %all-to-all-start.6) | async-done | bytes 65568 | tf_op jit(solution)/shard_map/all_to_all | solution.py:147
  237.6 0.7 copy.97
  (59 shorter events, 18.9 us)
Async XLA Ops:
  2.2 21.1 %copy-start = (bf16[128,256]{1,0:T(8,128)(2,1)S(1)}, bf16[128,256]{1,0:T(8,128)(2,1)}, u32[]{:S(2)}) copy-start(bf16[128,256]{1,0:T(8,128)(2,1)} %param.8) | copy-start | bytes 196612
  2.2 30.3 %all-to-all-start.1 = ((bf16[32,8,128]{2,1,0:T(8,128)(2,1)}), bf16[32,8,128]{2,1,0:T(8,128)(2,1)S(1)}, u32[]{:S(2)}, u32[]{:S(2)}) async-start(bf16[32,8,128]{2,1,0:T(8,128)(2,1)} %bitcast.4), calls=%async_computation.1 | async-start | bytes 131072 | tf_op jit(solution)/shard_map/all_to_all | solution.py:127
  32.5 13.0 %all-to-all-start.2 = ((bf16[32,8,128]{2,1,0:T(8,128)(2,1)}), bf16[32,8,128]{2,1,0:T(8,128)(2,1)S(1)}, u32[]{:S(2)}, u32[]{:S(2)}) async-start(bf16[32,8,128]{2,1,0:T(8,128)(2,1)} %bitcast.8), calls=%async_computation.2 | async-start | bytes 131072 | tf_op jit(solution)/shard_map/all_to_all | solution.py:128
  36.3 0.8 copy-start.1
  45.5 13.0 %all-to-all-start.3 = ((bf16[32,8,128]{2,1,0:T(8,128)(2,1)}), bf16[32,8,128]{2,1,0:T(8,128)(2,1)S(1)}, u32[]{:S(2)}, u32[]{:S(2)}) async-start(bf16[32,8,128]{2,1,0:T(8,128)(2,1)} %bitcast.17), calls=%async_computation.3 | async-start | bytes 131072 | tf_op jit(solution)/shard_map/all_to_all | solution.py:129
  58.5 13.0 %all-to-all-start = ((bf16[32,8,128]{2,1,0:T(8,128)(2,1)}), bf16[32,8,128]{2,1,0:T(8,128)(2,1)S(1)}, u32[]{:S(2)}, u32[]{:S(2)}) async-start(bf16[32,8,128]{2,1,0:T(8,128)(2,1)} %bitcast.1), calls=%async_computation | async-start | bytes 131072 | tf_op jit(solution)/shard_map/all_to_all | solution.py:126
  72.3 9.0 %copy-start.2 = (bf16[128,256]{1,0:T(8,128)(2,1)S(1)}, bf16[128,256]{1,0:T(8,128)(2,1)}, u32[]{:S(2)}) copy-start(bf16[128,256]{1,0:T(8,128)(2,1)} %param.11) | copy-start | bytes 196612
  72.3 18.1 %all-to-all-start.4 = ((bf16[8,32,128]{2,0,1:T(8,128)(2,1)}), bf16[8,32,128]{2,0,1:T(8,128)(2,1)S(1)}, u32[]{:S(2)}, u32[]{:S(2)}) async-start(bf16[8,32,128]{2,0,1:T(8,128)(2,1)} %fusion.30), calls=%async_computation.4 | async-start | bytes 131072 | tf_op jit(solution)/shard_map/all_to_all | solution.py:132
  81.3 9.1 %copy-start.3 = (f32[256]{0:T(256)S(1)}, f32[256]{0:T(256)}, u32[]{:S(2)}) copy-start(f32[256]{0:T(256)} %param.10) | copy-start | bytes 3076
  211.6 13.0 %all-to-all-start.8 = ((bf16[8,32,128]{2,0,1:T(8,128)(2,1)}), bf16[8,32,128]{2,0,1:T(8,128)(2,1)S(1)}, u32[]{:S(2)}, u32[]{:S(2)}) async-start(bf16[8,32,128]{2,0,1:T(8,128)(2,1)} %get-tuple-element.22), calls=%async_computation.8 | async-start | bytes 131072 | tf_op jit(solution)/shard_map/all_to_all | solution.py:149
  224.6 13.0 %all-to-all-start.6 = ((bf16[8,32,128]{2,0,1:T(8,128)(2,1)}), bf16[8,32,128]{2,0,1:T(8,128)(2,1)S(1)}, u32[]{:S(2)}, u32[]{:S(2)}) async-start(bf16[8,32,128]{2,0,1:T(8,128)(2,1)} %fusion.32), calls=%async_computation.6 | async-start | bytes 131072 | tf_op jit(solution)/shard_map/all_to_all | solution.py:147
where the time goes:
time: 243 us; the launch traced here: 238 us
  blocking collectives  114 us (47%)
  starting transfers between devices  49.4 us (20%)
  waiting for transfers between devices  49 us (20%)
  matrix products  14.1 us (6%)
  local copies, waits for them, and re-layouts  7.82 us (3%)
  other arithmetic  3.03 us (1%)
    psum x1, blocking collectives, per_device(): lax.psum((jnp.sum(prod_wide * prod_wide, axis=1), jnp.sum(gained * prod_w...  89.7 us
    all_to_all x1, starting transfers between devices, per_device(): lax.all_to_all(key_proj.T, 'seq', split_axis=0, concat_axis=1, tiled=True)  21.1 us
    all_to_all x1, blocking collectives, per_device(): lax.all_to_all(grad_tokens.T, 'seq', split_axis=0, concat_axis=1, tiled=T...  12.1 us
    all_to_all x1, blocking collectives, per_device(): lax.all_to_all(grads_own[1], 'seq', split_axis=1, concat_axis=0, tiled=True)  12.1 us
    all_to_all x1, waiting for transfers between devices, per_device(): lax.all_to_all(product, 'seq', split_axis=1, concat_axis=0, tiled=True)  9.01 us
    all_to_all x1, starting transfers between devices, per_device(): lax.all_to_all(product, 'seq', split_axis=1, concat_axis=0, tiled=True)  8.98 us
    all_to_all x1, waiting for transfers between devices, per_device(): lax.all_to_all(grads_own[2], 'seq', split_axis=1, concat_axis=0, tiled=True)  8.43 us
    all_to_all x1, waiting for transfers between devices, per_device(): lax.all_to_all(filters, 'seq', split_axis=0, concat_axis=1, tiled=True)  8.31 us
  transfers between devices with their start and end apart: 7, of which 7 were waited for; matrix products, arithmetic and copies ran while one was open for 6% of the time, Pallas kernels for 0%

commit v1 on v0

v1 whole, which is shorter than its diff:
```python
import functools

import jax
import jax.numpy as jnp
import numpy as np
from jax import lax
from jax.experimental import pallas as pl
from jax.experimental.pallas import tpu as pltpu
from jax.sharding import PartitionSpec as P

D = 8192
EPSILON = 1e-05

BF16 = jnp.bfloat16
F32 = jnp.float32


def split_halves(table):
    high = table.astype(jnp.bfloat16)
    low = (table - high.astype(np.float64)).astype(jnp.bfloat16)
    return (high, low)


def make_tables(blocks, block, rows):
    length = blocks * block
    n1 = np.arange(blocks)
    k1 = np.arange(blocks)
    outer = np.exp(-2j * np.pi * np.outer(k1 + 0.25, n1) / blocks)
    stacked = np.concatenate([outer.real, outer.imag], axis=0)
    eye = np.eye(rows)
    first = np.kron(stacked, eye)
    last = np.kron(stacked.T, eye) / length
    twist = np.exp(-2j * np.pi * np.outer(k1 + 0.25, np.arange(block)) / length)
    twist = np.repeat(twist, rows, axis=0)
    angle = 2 * np.pi * (np.outer(np.arange(block), np.arange(block)) % block) / block
    inner = np.block([[np.cos(angle), -np.sin(angle)], [np.sin(angle), np.cos(angle)]])
    first_high, first_low = split_halves(first)
    last_high, last_low = split_halves(last)
    inner_high, inner_low = split_halves(inner)
    return {
        "first": np.stack([first_high, first_low]),
        "last": np.stack([last_high, last_low]),
        "inner": np.stack([inner_high, inner_low]),
        "twist": np.stack([twist.real, twist.imag]).astype(np.float32),
    }


def halves(wide):
    high = wide.astype(BF16)
    low = (wide - high.astype(F32)).astype(BF16)
    return (high, low)


def mul(left, right, flip=False):
    dims = (((1,), (1 if flip else 0,)), ((), ()))
    return lax.dot_general(left, right, dims, preferred_element_type=F32)


def to_values(signal, first, inner, twist):
    rows, width = signal.shape
    block = twist.shape[2]
    part = mul(first[0], signal) + mul(first[1], signal)
    turned = []
    for i in range(width // block):
        part_re = part[:rows, i * block : (i + 1) * block]
        part_im = part[rows:, i * block : (i + 1) * block]
        turned.append(
            jnp.concatenate(
                [part_re * twist[0] - part_im * twist[1], part_re * twist[1] + part_im * twist[0]],
                axis=1,
            )
        )
    high, low = halves(jnp.concatenate(turned, axis=0))
    values = mul(high, inner[0]) + (mul(high, inner[1]) + mul(low, inner[0]))
    return [
        (values[i * rows : (i + 1) * rows, :block], values[i * rows : (i + 1) * rows, block:])
        for i in range(width // block)
    ]


def to_signal(value_re, value_im, last, inner, twist):
    block = twist.shape[2]
    high, low = halves(jnp.concatenate([value_re, value_im], axis=1))
    back = mul(high, inner[0], True) + (mul(high, inner[1], True) + mul(low, inner[0], True))
    back_re, back_im = back[:, :block], back[:, block:]
    turned = jnp.concatenate(
        [back_re * twist[0] + back_im * twist[1], back_im * twist[0] - back_re * twist[1]], axis=0
    )
    high, low = halves(turned)
    return mul(last[0], high) + (mul(last[0], low) + mul(last[1], high))


def call(body, outs, *args, name):
    shapes = [jax.ShapeDtypeStruct(shape, dtype) for shape, dtype in outs]
    return pl.pallas_call(body, out_shape=shapes, name=name)(*args)


def source_body(key_ref, value_ref, filter_ref, out_ref):
    peers, double, block = out_ref.shape
    source = (key_ref[...].astype(F32) * value_ref[...].astype(F32)).astype(BF16).astype(F32)
    source = source.T.reshape(peers, double // 2, block)
    taps = filter_ref[...].astype(F32).reshape(peers, double // 2, block)
    out_ref[...] = jnp.concatenate([source, taps], axis=1).astype(BF16)


def turn_body(query_ref, grad_ref, gain_ref, query_out, gained_out):
    query_out[...] = query_ref[...].astype(F32).T.astype(BF16)
    gained_out[...] = (grad_ref[...].astype(F32) * gain_ref[...]).T


def convolve_body(packed_ref, first_ref, last_ref, inner_ref, twist_ref, out_ref, values_ref):
    peers, double, block = packed_ref.shape
    per = double // 2
    packed = packed_ref[...].astype(F32)
    source = packed[:, :per].reshape(peers * per, block)
    taps = packed[:, per:].reshape(peers * per, block)
    signal = jnp.concatenate([source, taps], axis=1).astype(BF16)
    (src_re, src_im), (tap_re, tap_im) = to_values(signal, first_ref, inner_ref, twist_ref)
    values_ref[0] = tap_re
    values_ref[1] = tap_im
    out = to_signal(
        src_re * tap_re - src_im * tap_im,
        src_re * tap_im + src_im * tap_re,
        last_ref,
        inner_ref,
        twist_ref,
    )
    out_ref[...] = out.reshape(peers, per, block).astype(BF16)


def correlate_body(
    weighted_ref, values_ref, first_ref, last_ref, inner_ref, twist_ref, out_ref
):
    peers, per, block = weighted_ref.shape
    signal = weighted_ref[...].astype(F32).reshape(peers * per, block).astype(BF16)
    ((sig_re, sig_im),) = to_values(signal, first_ref, inner_ref, twist_ref)
    tap_re, tap_im = values_ref[0], values_ref[1]
    out = to_signal(
        sig_re * tap_re + sig_im * tap_im,
        sig_im * tap_re - sig_re * tap_im,
        last_ref,
        inner_ref,
        twist_ref,
    )
    out_ref[...] = out.reshape(peers, per, block).astype(BF16)


def product_of(conv_ref, query_ref):
    peers, per, block = conv_ref.shape
    conv = conv_ref[...].astype(F32).reshape(peers * per, block)
    query = query_ref[...].astype(F32)
    return (conv, query, (query * conv).astype(BF16).astype(F32))


def partial_body(conv_ref, query_ref, gained_ref, out_ref):
    _, _, product = product_of(conv_ref, query_ref)
    square = jnp.sum(product * product, axis=0, keepdims=True)
    cross = jnp.sum(gained_ref[...] * product, axis=0, keepdims=True)
    both = jnp.concatenate([square, cross], axis=0)
    out_ref[...] = jnp.broadcast_to(both[None], out_ref.shape)


def token_scales(sums_ref, width):
    sums = jnp.sum(sums_ref[...], axis=0)
    scale = lax.rsqrt(sums[0:1] / width + EPSILON)
    return (scale, sums[1:2] * scale * scale * scale / width)


def weighted_body(sums_ref, conv_ref, query_ref, gained_ref, weighted_ref, grad_ref, *, width):
    scale, pull = token_scales(sums_ref, width)
    _, query, product = product_of(conv_ref, query_ref)
    grad = (gained_ref[...] * scale - product * pull).astype(BF16)
    grad_ref[...] = grad
    weighted = grad.astype(F32) * query
    weighted_ref[...] = weighted.reshape(weighted_ref.shape).astype(BF16)


def outputs_body(
    sums_ref, conv_ref, query_ref, grad_ref, gain_ref, normed_ref, query_grad_ref, *, width
):
    scale, _ = token_scales(sums_ref, width)
    conv, _, product = product_of(conv_ref, query_ref)
    normed_ref[...] = ((product * scale).T * gain_ref[...]).astype(BF16)
    query_grad_ref[...] = (grad_ref[...].astype(F32) * conv).T.astype(BF16)


def finish_body(spread_ref, key_ref, value_ref, key_grad_ref, value_grad_ref):
    peers, per, block = spread_ref.shape
    spread = spread_ref[...].astype(F32).reshape(peers * per, block).T
    key_grad_ref[...] = (spread * value_ref[...].astype(F32)).astype(BF16)
    value_grad_ref[...] = (spread * key_ref[...].astype(F32)).astype(BF16)


def per_device(query, key, value, filters, gain, out_grad):
    peers = lax.axis_size("seq")
    groups = lax.axis_size("chan")
    block, wide = query.shape
    per = wide // peers
    width = float(wide * groups)
    tables = make_tables(peers, block, per)
    first, last, inner, twist = (
        jnp.asarray(tables[name]) for name in ("first", "last", "inner", "twist")
    )
    gain = gain.reshape(1, wide)

    def exchange(array, axis="seq"):
        return lax.all_to_all(array, axis, split_axis=0, concat_axis=0, tiled=True)

    (packed,) = call(
        source_body, [((peers, 2 * per, block), BF16)], key, value, filters, name="source"
    )
    packed = exchange(packed)
    query_t, gained_t = call(
        turn_body, [((wide, block), BF16), ((wide, block), F32)], query, out_grad, gain, name="turn"
    )
    conv, values = call(
        convolve_body,
        [((peers, per, block), BF16), ((2, wide, block), F32)],
        packed,
        first,
        last,
        inner,
        twist,
        name="convolve",
    )
    conv = exchange(conv)
    (partial,) = call(
        partial_body, [((groups, 2, block), F32)], conv, query_t, gained_t, name="partial"
    )
    sums = exchange(partial, "chan")
    weighted, grad = call(
        functools.partial(weighted_body, width=width),
        [((peers, per, block), BF16), ((wide, block), BF16)],
        sums,
        conv,
        query_t,
        gained_t,
        name="weighted",
    )
    weighted = exchange(weighted)
    normed, query_grad = call(
        functools.partial(outputs_body, width=width),
        [((block, wide), BF16), ((block, wide), BF16)],
        sums,
        conv,
        query_t,
        grad,
        gain,
        name="outputs",
    )
    (spread,) = call(
        correlate_body,
        [((peers, per, block), BF16)],
        weighted,
        values,
        first,
        last,
        inner,
        twist,
        name="correlate",
    )
    spread = exchange(spread)
    key_grad, value_grad = call(
        finish_body,
        [((block, wide), BF16), ((block, wide), BF16)],
        spread,
        key,
        value,
        name="finish",
    )
    return (normed, query_grad, key_grad, value_grad)


def solution(mesh):
    tokens = P("seq", "chan")
    return jax.shard_map(
        per_device,
        mesh=mesh,
        in_specs=(tokens, tokens, tokens, P("chan", "seq"), P("chan"), tokens),
        out_specs=(tokens, tokens, tokens, tokens),
        check_vma=False,
    )
```

time: 243 us -> 112 us (0.46); the launches traced: 238 us -> 111 us
  blocking collectives: 114 us -> 68.8 us
  starting transfers between devices: 49.4 us -> 8.19 us
  waiting for transfers between devices: 49 us -> 15.1 us
  Pallas kernels: 0 us -> 17 us
  matrix products: 14.1 us -> 0 us
  local copies, waits for them, and re-layouts: 7.82 us -> 1.25 us
  other arithmetic: 3.03 us -> 0 us
    psum x1 -> x0, blocking collectives: 89.7 us -> none  [per_device(): lax.psum((jnp.sum(prod_wide * prod_wide, axis=1), jnp.sum(gained * prod_w...]
    all_to_all x2 -> x3, blocking collectives: 24.2 us -> 68.8 us  [exchange(): return lax.all_to_all(array, axis, split_axis=0, concat_axis=0, tiled=True)]
    all_to_all x7 -> x2, starting transfers between devices: 49.4 us -> 8.19 us  [exchange(): return lax.all_to_all(array, axis, split_axis=0, concat_axis=0, tiled=True)]
    all_to_all x7 -> x2, waiting for transfers between devices: 49 us -> 15.1 us  [exchange(): return lax.all_to_all(array, axis, split_axis=0, concat_axis=0, tiled=True)]
    pallas_call x0 -> x8, Pallas kernels: none -> 17 us  [call(): return pl.pallas_call(body, out_shape=shapes, name=name)(*args)]
    dot_general x28 -> x0, matrix products: 13.6 us -> none  [the longest x3 1.78 us: forward_real(): jnp.einsum('bkn,jn->bkj', turned_im, inner_dft[0], precision=HIGHEST)]
    unnamed x16 -> x4, local copies, waits for them, and re-layouts: 6.7 us -> 1.25 us
  transfers between devices with their start and end apart: 7 -> 2, of which waited for: 7 -> 2; matrix products, arithmetic and copies ran while one was open for 6% -> 0% of each run, Pallas kernels for 0% -> 3%
where the time goes in v1:
time: 112 us; the launch traced here: 111 us
  blocking collectives  68.8 us (61%)
  Pallas kernels  17 us (15%)
  waiting for transfers between devices  15.1 us (13%)
  starting transfers between devices  8.19 us (7%)
  local copies, waits for them, and re-layouts  1.25 us (1%)
    all_to_all x3, blocking collectives, exchange(): return lax.all_to_all(array, axis, split_axis=0, concat_axis=0, tiled=True)  68.8 us
    pallas_call x8, Pallas kernels, call(): return pl.pallas_call(body, out_shape=shapes, name=name)(*args)  17 us
    all_to_all x2, waiting for transfers between devices, exchange(): return lax.all_to_all(array, axis, split_axis=0, concat_axis=0, tiled=True)  15.1 us
    all_to_all x2, starting transfers between devices, exchange(): return lax.all_to_all(array, axis, split_axis=0, concat_axis=0, tiled=True)  8.19 us
  transfers between devices with their start and end apart: 2, of which 2 were waited for; matrix products, arithmetic and copies ran while one was open for 0% of the time, Pallas kernels for 3%

profile of v1, /device:TPU:1, one launch (start us, length us, event | category | flops | bytes accessed | tf_op | source)
XLA Modules:
  0.0 111.0 jit_solution(15604827057720417184)
XLA Ops:
  0.6 1.7 %source.1 = bf16[32,16,128]{2,1,0:T(8,128)(2,1)} custom-call(bf16[128,256]{1,0:T(8,128)(2,1)} %key_ref.3, bf16[128,256]{1,0:T(8,128)(2,1)} %value_ref.3, bf16[256,128]{1,0:T(8,128)(2,1)} %filter_ref.1), custom_call_target="tpu_custom_call" | custom-call | tf_op jit(solution)/shard_map/source/pallas_call | solution.py:95
  2.3 30.4 %all_to_all.25.packed_ref = bf16[32,16,128]{2,1,0:T(8,128)(2,1)} all-to-all(bf16[32,16,128]{2,1,0:T(8,128)(2,1)} %source.1), channel_id=1, replica_groups=mesh['seq'=32,'chan'=32] {'seq'}, dimensions={0} | all-to-all | bytes 262144 | tf_op jit(solution)/shard_map/all_to_all | solution.py:207
  32.7 3.5 %convolve.1 = (bf16[32,8,128]{2,1,0:T(8,128)(2,1)}, f32[2,256,128]{2,1,0:T(8,128)}) custom-call(bf16[32,16,128]{2,1,0:T(8,128)(2,1)} %all_to_all.25.packed_ref, bf16[2,512,256]{2,1,0:T(8,128)(2,1)} %constant.8.clone.first_ref, bf16[2,256,512]{2,1,0:T(8,128)(2,1)} %constant.9.clone.last_ref, bf16[2,256,256]{2,1,0:T(8,128)(2,1)} %constant.10.clone.inner_ref, ...), custom_call_target="tpu_custom_call" | custom-call | tf_op jit(solution)/shard_map/convolve/pallas_call | solution.py:95
  36.2 4.4 %all-to-all-start.1 = ((bf16[32,8,128]{2,1,0:T(8,128)(2,1)}), bf16[32,8,128]{2,1,0:T(8,128)(2,1)S(1)}, u32[]{:S(2)}, u32[]{:S(2)}) async-start(bf16[32,8,128]{2,1,0:T(8,128)(2,1)} %get-tuple-element.14), calls=%async_computation.1 | async-start | bytes 131072 | tf_op jit(solution)/shard_map/all_to_all | solution.py:207
  40.6 1.7 %turn.1 = (bf16[256,128]{1,0:T(8,128)(2,1)}, f32[256,128]{1,0:T(8,128)}) custom-call(bf16[128,256]{1,0:T(8,128)(2,1)} %query_ref.1, bf16[128,256]{1,0:T(8,128)(2,1)} %grad_ref.1, f32[1,256]{1,0:T(1,128)} %bitcast.1), custom_call_target="tpu_custom_call" | custom-call | tf_op jit(solution)/shard_map/turn/pallas_call | solution.py:95
  42.2 7.6 %all-to-all-done.1.conv_ref = bf16[32,8,128]{2,1,0:T(8,128)(2,1)S(1)} async-done(((bf16[32,8,128]{2,1,0:T(8,128)(2,1)}), bf16[32,8,128]{2,1,0:T(8,128)(2,1)S(1)}, u32[]{:S(2)}, u32[]{:S(2)}) %all-to-all-start.1) | async-done | bytes 65568 | tf_op jit(solution)/shard_map/all_to_all | solution.py:207
  49.8 0.0 copy-start
  49.8 0.6 copy-done
  50.5 1.6 %partial.1 = f32[32,2,128]{2,1,0:T(2,128)} custom-call(bf16[32,8,128]{2,1,0:T(8,128)(2,1)} %copy-done, bf16[256,128]{1,0:T(8,128)(2,1)} %get-tuple-element.15.query_ref, f32[256,128]{1,0:T(8,128)} %get-tuple-element.16.gained_ref), custom_call_target="tpu_custom_call" | custom-call | tf_op jit(solution)/shard_map/partial/pallas_call | solution.py:95
  52.1 24.7 %all_to_all.26.sums_ref = f32[32,2,128]{2,1,0:T(2,128)} all-to-all(f32[32,2,128]{2,1,0:T(2,128)} %partial.1), channel_id=1, replica_groups=mesh['seq'=32,'chan'=32] {'chan'}, dimensions={0} | all-to-all | bytes 65536 | tf_op jit(solution)/shard_map/all_to_all | solution.py:207
  76.8 1.7 %weighted.1 = (bf16[32,8,128]{2,1,0:T(8,128)(2,1)}, bf16[256,128]{1,0:T(8,128)(2,1)}) custom-call(f32[32,2,128]{2,1,0:T(2,128)} %all_to_all.26.sums_ref, bf16[32,8,128]{2,1,0:T(8,128)(2,1)} %copy-done, bf16[256,128]{1,0:T(8,128)(2,1)} %get-tuple-element.15.query_ref, f32[256,128]{1,0:T(8,128)} %get-tuple-element.16.gained_ref), custom_call_target="tpu_custom_call" | custom-call | tf_op jit(solution)/shard_map/weighted/pallas_call | solution.py:95
  78.5 13.7 %all_to_all.27.weighted_ref = bf16[32,8,128]{2,1,0:T(8,128)(2,1)} all-to-all(bf16[32,8,128]{2,1,0:T(8,128)(2,1)} %get-tuple-element.20), channel_id=1, replica_groups=mesh['seq'=32,'chan'=32] {'seq'}, dimensions={0} | all-to-all | bytes 131072 | tf_op jit(solution)/shard_map/all_to_all | solution.py:207
  92.2 3.4 %correlate.1 = bf16[32,8,128]{2,1,0:T(8,128)(2,1)} custom-call(bf16[32,8,128]{2,1,0:T(8,128)(2,1)} %all_to_all.27.weighted_ref, f32[2,256,128]{2,1,0:T(8,128)} %get-tuple-element.21.values_ref, bf16[2,512,256]{2,1,0:T(8,128)(2,1)} %constant.8.clone.first_ref, bf16[2,256,512]{2,1,0:T(8,128)(2,1)} %constant.9.clone.last_ref, ...), custom_call_target="tpu_custom_call" | custom-call | tf_op jit(solution)/shard_map/correlate/pallas_call | solution.py:95
  95.7 3.8 %all-to-all-start.4 = ((bf16[32,8,128]{2,1,0:T(8,128)(2,1)}), bf16[32,8,128]{2,1,0:T(8,128)(2,1)S(1)}, u32[]{:S(2)}, u32[]{:S(2)}) async-start(bf16[32,8,128]{2,1,0:T(8,128)(2,1)} %correlate.1), calls=%async_computation.4 | async-start | bytes 131072 | tf_op jit(solution)/shard_map/all_to_all | solution.py:207
  99.5 1.7 %outputs.1 = (bf16[128,256]{1,0:T(8,128)(2,1)}, bf16[128,256]{1,0:T(8,128)(2,1)}) custom-call(f32[32,2,128]{2,1,0:T(2,128)} %all_to_all.26.sums_ref, bf16[32,8,128]{2,1,0:T(8,128)(2,1)} %copy-done, bf16[256,128]{1,0:T(8,128)(2,1)} %get-tuple-element.15.query_ref, bf16[256,128]{1,0:T(8,128)(2,1)} %get-tuple-element.17.grad_ref, f32[1,256]{1,0:T(1,128)} %bitcast.2), custom_call_target="tpu_custom_call" | custom-call | tf_op jit(solution)/shard_map/outputs/pallas_call | solution.py:95
  101.2 7.5 %all-to-all-done.4.spread_ref = bf16[32,8,128]{2,1,0:T(8,128)(2,1)S(1)} async-done(((bf16[32,8,128]{2,1,0:T(8,128)(2,1)}), bf16[32,8,128]{2,1,0:T(8,128)(2,1)S(1)}, u32[]{:S(2)}, u32[]{:S(2)}) %all-to-all-start.4) | async-done | bytes 65568 | tf_op jit(solution)/shard_map/all_to_all | solution.py:207
  108.7 0.0 copy-start.1
  108.7 0.6 copy-done.1
  109.4 1.7 %finish.1 = (bf16[128,256]{1,0:T(8,128)(2,1)}, bf16[128,256]{1,0:T(8,128)(2,1)}) custom-call(bf16[32,8,128]{2,1,0:T(8,128)(2,1)} %copy-done.1, bf16[128,256]{1,0:T(8,128)(2,1)} %key_ref.3, bf16[128,256]{1,0:T(8,128)(2,1)} %value_ref.3), custom_call_target="tpu_custom_call" | custom-call | tf_op jit(solution)/shard_map/finish/pallas_call | solution.py:95
Async XLA Ops:
  36.2 13.6 %all-to-all-start.1 = ((bf16[32,8,128]{2,1,0:T(8,128)(2,1)}), bf16[32,8,128]{2,1,0:T(8,128)(2,1)S(1)}, u32[]{:S(2)}, u32[]{:S(2)}) async-start(bf16[32,8,128]{2,1,0:T(8,128)(2,1)} %get-tuple-element.14), calls=%async_computation.1 | async-start | bytes 131072 | tf_op jit(solution)/shard_map/all_to_all | solution.py:207
  49.8 0.6 copy-start
  95.7 13.1 %all-to-all-start.4 = ((bf16[32,8,128]{2,1,0:T(8,128)(2,1)}), bf16[32,8,128]{2,1,0:T(8,128)(2,1)S(1)}, u32[]{:S(2)}, u32[]{:S(2)}) async-start(bf16[32,8,128]{2,1,0:T(8,128)(2,1)} %correlate.1), calls=%async_computation.4 | async-start | bytes 131072 | tf_op jit(solution)/shard_map/all_to_all | solution.py:207
  108.7 0.6 copy-start.1

commit v2 on v1

v2 whole, which is shorter than its diff:
```python
import functools

import jax
import jax.numpy as jnp
import numpy as np
from jax import lax
from jax.experimental import pallas as pl
from jax.experimental.pallas import tpu as pltpu
from jax.sharding import PartitionSpec as P

D = 8192
EPSILON = 1e-05

BF16 = jnp.bfloat16
F32 = jnp.float32
VMEM_LIMIT = 24 << 20


def split_halves(table):
    high = table.astype(jnp.bfloat16)
    low = (table - high.astype(np.float64)).astype(jnp.bfloat16)
    return [high, low]


def make_table(blocks, block, rows):
    length = blocks * block
    steps = np.arange(blocks)
    outer = np.exp(-2j * np.pi * np.outer(steps + 0.25, steps) / blocks)
    eye = np.eye(rows)
    first = np.kron(np.concatenate([outer.real, outer.imag], axis=0), eye)
    last = [np.kron(part.T, eye) / length for part in (outer.real, outer.imag)]
    twist = np.exp(-2j * np.pi * np.outer(steps + 0.25, np.arange(block)) / length)
    twist = np.repeat(np.concatenate([twist.real, twist.imag], axis=1), rows, axis=0)
    angle = 2 * np.pi * (np.outer(np.arange(block), np.arange(block)) % block) / block
    inner = np.block([[np.cos(angle), -np.sin(angle)], [np.sin(angle), np.cos(angle)]])
    parts = split_halves(first) + split_halves(inner) + split_halves(twist)
    parts = parts + split_halves(last[0]) + split_halves(last[1])
    return np.concatenate(parts, axis=0)


class Table:
    def __init__(self, ref):
        self.ref = ref
        self.size = ref.shape[1]
        self.block = self.size // 2
        size = self.size
        self.first = [(0, 2 * size), (2 * size, 2 * size)]
        self.inner = [(4 * size, size), (5 * size, size)]
        self.twist = [(6 * size, size), (7 * size, size)]
        self.last = [[(8 * size, size), (9 * size, size)], [(10 * size, size), (11 * size, size)]]

    def rows(self, span):
        return self.ref[span[0] : span[0] + span[1], :]

    def turns(self):
        wide = self.rows(self.twist[0]).astype(F32) + self.rows(self.twist[1]).astype(F32)
        return (wide[:, : self.block], wide[:, self.block :])


def halves(wide):
    high = wide.astype(BF16)
    low = (wide - high.astype(F32)).astype(BF16)
    return (high, low)


def mul(left, right, flip=False):
    dims = (((1,), (1 if flip else 0,)), ((), ()))
    return lax.dot_general(left, right, dims, preferred_element_type=F32)


def to_values(signal, table, turn_re, turn_im):
    rows, width = signal.shape
    block = table.block
    part = mul(table.rows(table.first[0]), signal) + mul(table.rows(table.first[1]), signal)
    turned = []
    for i in range(width // block):
        part_re = part[:rows, i * block : (i + 1) * block]
        part_im = part[rows:, i * block : (i + 1) * block]
        turned.append(
            jnp.concatenate(
                [part_re * turn_re - part_im * turn_im, part_re * turn_im + part_im * turn_re],
                axis=1,
            )
        )
    high, low = halves(jnp.concatenate(turned, axis=0))
    inner = [table.rows(span) for span in table.inner]
    values = mul(high, inner[0]) + (mul(high, inner[1]) + mul(low, inner[0]))
    return [
        (values[i * rows : (i + 1) * rows, :block], values[i * rows : (i + 1) * rows, block:])
        for i in range(width // block)
    ]


def to_signal(value_re, value_im, table, turn_re, turn_im):
    block = table.block
    high, low = halves(jnp.concatenate([value_re, value_im], axis=1))
    inner = [table.rows(span) for span in table.inner]
    back = mul(high, inner[0], True) + (mul(high, inner[1], True) + mul(low, inner[0], True))
    back_re, back_im = back[:, :block], back[:, block:]
    turned = (back_re * turn_re + back_im * turn_im, back_im * turn_re - back_re * turn_im)
    out = None
    for wide, (span_high, span_low) in zip(turned, table.last):
        high, low = halves(wide)
        last = table.rows(span_high)
        term = mul(last, high) + (mul(last, low) + mul(table.rows(span_low), high))
        out = term if out is None else out + term
    return out


def call(body, name, args, outs, scratch=()):
    whole = pl.BlockSpec(memory_space=pltpu.VMEM)
    apart = pl.BlockSpec(memory_space=pltpu.HBM)
    return pl.pallas_call(
        body,
        out_shape=[
            (pltpu.VMEM if keep else pltpu.HBM)(shape, dtype)
            for shape, dtype, keep in outs
        ],
        in_specs=[whole if keep else apart for _, keep in args],
        out_specs=[whole if keep else apart for _, _, keep in outs],
        scratch_shapes=list(scratch),
        compiler_params=pltpu.CompilerParams(vmem_limit_bytes=VMEM_LIMIT),
        name=name,
    )(
        *[
            pltpu.with_memory_space_constraint(x, pltpu.VMEM if keep else pltpu.HBM)
            for x, keep in args
        ]
    )


def source_body(
    key_hbm,
    value_hbm,
    filter_hbm,
    query_hbm,
    grad_hbm,
    gain_hbm,
    table_hbm,
    packed_ref,
    key_ref,
    value_ref,
    query_ref,
    grad_ref,
    gain_ref,
    table_ref,
    filter_ref,
    sems,
):
    pairs = [
        (key_hbm, key_ref),
        (value_hbm, value_ref),
        (filter_hbm, filter_ref),
        (query_hbm, query_ref),
        (grad_hbm, grad_ref),
        (gain_hbm, gain_ref),
        (table_hbm, table_ref),
    ]
    copies = [pltpu.make_async_copy(a, b, sems.at[i]) for i, (a, b) in enumerate(pairs)]
    for copy in copies:
        copy.start()
    for copy in copies[:3]:
        copy.wait()
    peers, double, block = packed_ref.shape
    source = (key_ref[...].astype(F32) * value_ref[...].astype(F32)).astype(BF16).astype(F32)
    source = source.T.reshape(peers, double // 2, block)
    taps = filter_ref[...].astype(F32).reshape(peers, double // 2, block)
    packed_ref[...] = jnp.concatenate([source, taps], axis=1).astype(BF16)
    for copy in copies[3:]:
        copy.wait()


def convolve_body(
    packed_ref,
    query_ref,
    grad_ref,
    gain_ref,
    table_ref,
    out_ref,
    values_ref,
    query_t_ref,
    gained_t_ref,
):
    table = Table(table_ref)
    turns = table.turns()
    peers, double, block = packed_ref.shape
    per = double // 2
    packed = packed_ref[...].astype(F32)
    source = packed[:, :per].reshape(peers * per, block)
    taps = packed[:, per:].reshape(peers * per, block)
    signal = jnp.concatenate([source, taps], axis=1).astype(BF16)
    (src_re, src_im), (tap_re, tap_im) = to_values(signal, table, *turns)
    values_ref[0] = tap_re
    values_ref[1] = tap_im
    query_t_ref[...] = query_ref[...].astype(F32).T.astype(BF16)
    gained_t_ref[...] = (grad_ref[...].astype(F32) * gain_ref[...]).T
    out = to_signal(
        src_re * tap_re - src_im * tap_im, src_re * tap_im + src_im * tap_re, table, *turns
    )
    out_ref[...] = out.reshape(peers, per, block).astype(BF16)


def product_of(conv_ref, query_ref):
    peers, per, block = conv_ref.shape
    conv = conv_ref[...].astype(F32).reshape(peers * per, block)
    query = query_ref[...].astype(F32)
    return (conv, query, (query * conv).astype(BF16).astype(F32))


def partial_body(conv_ref, query_ref, gained_ref, out_ref):
    _, _, product = product_of(conv_ref, query_ref)
    square = jnp.sum(product * product, axis=0, keepdims=True)
    cross = jnp.sum(gained_ref[...] * product, axis=0, keepdims=True)
    both = jnp.concatenate([square, cross], axis=0)
    out_ref[...] = jnp.broadcast_to(both[None], out_ref.shape)


def token_scales(sums_ref, width):
    sums = jnp.sum(sums_ref[...], axis=0)
    scale = lax.rsqrt(sums[0:1] / width + EPSILON)
    return (scale, sums[1:2] * scale * scale * scale / width)


def weighted_body(
    sums_ref, conv_ref, query_ref, gained_ref, weighted_ref, grad_ref, scaled_ref, *, width
):
    scale, pull = token_scales(sums_ref, width)
    conv, query, product = product_of(conv_ref, query_ref)
    scaled = product * scale
    grad = (gained_ref[...] * scale - product * pull).astype(BF16).astype(F32)
    weighted_ref[...] = (grad * query).reshape(weighted_ref.shape).astype(BF16)
    scaled_ref[...] = scaled
    grad_ref[...] = (grad * conv).astype(BF16)


def correlate_body(
    weighted_ref,
    values_ref,
    scaled_ref,
    grad_ref,
    gain_ref,
    table_ref,
    out_ref,
    normed_hbm,
    query_grad_hbm,
    normed_ref,
    query_grad_ref,
    sems,
):
    normed_ref[...] = (scaled_ref[...].T * gain_ref[...]).astype(BF16)
    query_grad_ref[...] = grad_ref[...].astype(F32).T.astype(BF16)
    copies = [
        pltpu.make_async_copy(normed_ref, normed_hbm, sems.at[0]),
        pltpu.make_async_copy(query_grad_ref, query_grad_hbm, sems.at[1]),
    ]
    for copy in copies:
        copy.start()
    table = Table(table_ref)
    turns = table.turns()
    peers, per, block = weighted_ref.shape
    signal = weighted_ref[...].astype(F32).reshape(peers * per, block).astype(BF16)
    ((sig_re, sig_im),) = to_values(signal, table, *turns)
    tap_re, tap_im = values_ref[0], values_ref[1]
    out = to_signal(
        sig_re * tap_re + sig_im * tap_im, sig_im * tap_re - sig_re * tap_im, table, *turns
    )
    out_ref[...] = out.reshape(peers, per, block).astype(BF16)
    for copy in copies:
        copy.wait()


def finish_body(
    spread_ref, key_ref, value_ref, key_hbm, value_hbm, key_grad_ref, value_grad_ref, sems
):
    peers, per, block = spread_ref.shape
    spread = spread_ref[...].astype(F32).reshape(peers * per, block).T
    key_grad_ref[...] = (spread * value_ref[...].astype(F32)).astype(BF16)
    first = pltpu.make_async_copy(key_grad_ref, key_hbm, sems.at[0])
    first.start()
    value_grad_ref[...] = (spread * key_ref[...].astype(F32)).astype(BF16)
    second = pltpu.make_async_copy(value_grad_ref, value_hbm, sems.at[1])
    second.start()
    first.wait()
    second.wait()


def per_device(query, key, value, filters, gain, out_grad):
    peers = lax.axis_size("seq")
    groups = lax.axis_size("chan")
    block, wide = query.shape
    per = wide // peers
    width = float(wide * groups)
    table = jnp.asarray(make_table(peers, block, per))
    gain = gain.reshape(1, wide)
    home = (block, wide)
    turned = (wide, block)
    owned = (peers, per, block)

    def exchange(array, axis="seq"):
        return lax.all_to_all(array, axis, split_axis=0, concat_axis=0, tiled=True)

    def dma(count):
        return pltpu.SemaphoreType.DMA((count,))

    packed, key, value, query, out_grad, gain, table = call(
        source_body,
        "source",
        [(x, False) for x in (key, value, filters, query, out_grad, gain, table)],
        [((peers, 2 * per, block), BF16, True)]
        + [(home, BF16, True)] * 4
        + [((1, wide), F32, True), (table.shape, BF16, True)],
        [pltpu.VMEM(turned, BF16), dma(7)],
    )
    packed = exchange(packed)
    conv, values, query_t, gained_t = call(
        convolve_body,
        "convolve",
        [(x, True) for x in (packed, query, out_grad, gain, table)],
        [
            (owned, BF16, True),
            ((2, wide, block), F32, True),
            (turned, BF16, True),
            (turned, F32, True),
        ],
    )
    conv = exchange(conv)
    (partial,) = call(
        partial_body,
        "partial",
        [(x, True) for x in (conv, query_t, gained_t)],
        [((groups, 2, block), F32, True)],
    )
    sums = exchange(partial, "chan")
    weighted, grad, scaled = call(
        functools.partial(weighted_body, width=width),
        "weighted",
        [(x, True) for x in (sums, conv, query_t, gained_t)],
        [(owned, BF16, True), (turned, BF16, True), (turned, F32, True)],
    )
    weighted = exchange(weighted)
    spread, normed, query_grad = call(
        correlate_body,
        "correlate",
        [(x, True) for x in (weighted, values, scaled, grad, gain, table)],
        [(owned, BF16, True), (home, BF16, False), (home, BF16, False)],
        [pltpu.VMEM(home, BF16), pltpu.VMEM(home, BF16), dma(2)],
    )
    spread = exchange(spread)
    key_grad, value_grad = call(
        finish_body,
        "finish",
        [(x, True) for x in (spread, key, value)],
        [(home, BF16, False), (home, BF16, False)],
        [pltpu.VMEM(home, BF16), pltpu.VMEM(home, BF16), dma(2)],
    )
    return (normed, query_grad, key_grad, value_grad)


def solution(mesh):
    tokens = P("seq", "chan")
    return jax.shard_map(
        per_device,
        mesh=mesh,
        in_specs=(tokens, tokens, tokens, P("chan", "seq"), P("chan"), tokens),
        out_specs=(tokens, tokens, tokens, tokens),
        check_vma=False,
    )
```

time: 112 us -> 99 us (0.88)
  blocking collectives: 68.8 us -> 91.7 us
  waiting for transfers between devices: 15.1 us -> 0 us
  Pallas kernels: 17 us -> 6.03 us
  starting transfers between devices: 8.19 us -> 0 us
  local copies, waits for them, and re-layouts: 1.25 us -> 0 us
    all_to_all x3 -> x5, blocking collectives: 68.8 us -> 91.7 us  [exchange(): return lax.all_to_all(array, axis, split_axis=0, concat_axis=0, tiled=True)]
    all_to_all x2 -> x0, waiting for transfers between devices: 15.1 us -> none  [exchange(): return lax.all_to_all(array, axis, split_axis=0, concat_axis=0, tiled=True)]
    pallas_call x8 -> x6, Pallas kernels: 17 us -> 6.03 us  [call(): pl.pallas_call(body, out_shape=[(pltpu.VMEM if keep else pltpu.HBM)(shape...]
    all_to_all x2 -> x0, starting transfers between devices: 8.19 us -> none  [exchange(): return lax.all_to_all(array, axis, split_axis=0, concat_axis=0, tiled=True)]
    unnamed x4 -> x0, local copies, waits for them, and re-layouts: 1.25 us -> none
  transfers between devices with their start and end apart: 2 -> 0, of which waited for: 2 -> 0; matrix products, arithmetic and copies ran while one was open for 0% -> 0% of each run, Pallas kernels for 3% -> 0%
where the time goes in v2:
time: 99 us; the launch traced here: 98.4 us
  blocking collectives  91.7 us (93%)
  Pallas kernels  6.03 us (6%)
    all_to_all x5, blocking collectives, exchange(): return lax.all_to_all(array, axis, split_axis=0, concat_axis=0, tiled=True)  91.7 us
    pallas_call x6, Pallas kernels, call(): pl.pallas_call(body, out_shape=[(pltpu.VMEM if keep else pltpu.HBM)(shape...  6.03 us

profile of v2, /device:TPU:1, one launch (start us, length us, event | category | flops | bytes accessed | tf_op | source)
XLA Modules:
  0.0 98.4 jit_solution(4152851699921321391)
XLA Ops:
  0.6 1.7 %source.1 = (bf16[32,16,128]{2,1,0:T(8,128)(2,1)S(1)}, bf16[128,256]{1,0:T(8,128)(2,1)S(1)}, bf16[128,256]{1,0:T(8,128)(2,1)S(1)}, bf16[128,256]{1,0:T(8,128)(2,...) custom-call(bf16[128,256]{1,0:T(8,128)(2,1)} %key_hbm.1, ...), custom_call_target="tpu_custom_call" | custom-call | tf_op jit(solution)/shard_map/source/pallas_call | solution.py:113
  2.3 30.1 %all_to_all.25.packed_ref = bf16[32,16,128]{2,1,0:T(8,128)(2,1)S(1)} all-to-all(bf16[32,16,128]{2,1,0:T(8,128)(2,1)S(1)} %get-tuple-element.23), channel_id=1, replica_groups=mesh['seq'=32,'chan'=32] {'seq'}, dimensions={0} | all-to-all | bytes 262144 | tf_op jit(solution)/shard_map/all_to_all | solution.py:300
  32.5 1.5 %convolve.1 = (bf16[32,8,128]{2,1,0:T(8,128)(2,1)S(1)}, f32[2,256,128]{2,1,0:T(8,128)S(1)}, bf16[256,128]{1,0:T(8,128)(2,1)S(1)}, f32[256,128]{1,0:T(8,128)S(1)}) custom-call(bf16[32,16,128]{2,1,0:T(8,128)(2,1)S(1)} %all_to_all.25.packed_ref, bf16[128,256]{1,0:T(8,128)(2,1)S(1)} %get-tuple-element.24.query_ref, ...), custom_call_target="tpu_custom_call" | custom-call | tf_op jit(solution)/shard_map/convolve/pallas_call | solution.py:113
  33.9 13.3 %all_to_all.26.conv_ref = bf16[32,8,128]{2,1,0:T(8,128)(2,1)S(1)} all-to-all(bf16[32,8,128]{2,1,0:T(8,128)(2,1)S(1)} %get-tuple-element.28), channel_id=1, replica_groups=mesh['seq'=32,'chan'=32] {'seq'}, dimensions={0} | all-to-all | bytes 131072 | tf_op jit(solution)/shard_map/all_to_all | solution.py:300
  47.2 0.1 partial.1
  47.3 23.9 %all_to_all.27.sums_ref = f32[32,2,128]{2,1,0:T(2,128)S(1)} all-to-all(f32[32,2,128]{2,1,0:T(2,128)S(1)} %partial.1), channel_id=1, replica_groups=mesh['seq'=32,'chan'=32] {'chan'}, dimensions={0} | all-to-all | bytes 65536 | tf_op jit(solution)/shard_map/all_to_all | solution.py:300
  71.2 0.1 weighted.1
  71.3 12.1 %all_to_all.28.weighted_ref = bf16[32,8,128]{2,1,0:T(8,128)(2,1)S(1)} all-to-all(bf16[32,8,128]{2,1,0:T(8,128)(2,1)S(1)} %get-tuple-element.31), channel_id=1, replica_groups=mesh['seq'=32,'chan'=32] {'seq'}, dimensions={0} | all-to-all | bytes 131072 | tf_op jit(solution)/shard_map/all_to_all | solution.py:300
  83.5 1.9 %correlate.1 = (bf16[32,8,128]{2,1,0:T(8,128)(2,1)S(1)}, bf16[128,256]{1,0:T(8,128)(2,1)}, bf16[128,256]{1,0:T(8,128)(2,1)}) custom-call(bf16[32,8,128]{2,1,0:T(8,128)(2,1)S(1)} %all_to_all.28.weighted_ref, f32[2,256,128]{2,1,0:T(8,128)S(1)} %get-tuple-element.32.values_ref, f32[256,128]{1,0:T(8,128)S(1)} %get-tuple-element.33.scaled_ref, ...), custom_call_target="tpu_custom_call" | custom-call | tf_op jit(solution)/shard_map/correlate/pallas_call | solution.py:113
  85.4 12.2 %all_to_all.29.spread_ref = bf16[32,8,128]{2,1,0:T(8,128)(2,1)S(1)} all-to-all(bf16[32,8,128]{2,1,0:T(8,128)(2,1)S(1)} %get-tuple-element.37), channel_id=1, replica_groups=mesh['seq'=32,'chan'=32] {'seq'}, dimensions={0} | all-to-all | bytes 131072 | tf_op jit(solution)/shard_map/all_to_all | solution.py:300
  97.6 0.8 finish.1

commit v3 on v2

v3 whole, which is shorter than its diff:
```python
import functools

import jax
import jax.numpy as jnp
import numpy as np
from jax import lax
from jax.experimental import pallas as pl
from jax.experimental.pallas import tpu as pltpu
from jax.sharding import PartitionSpec as P

D = 8192
EPSILON = 1e-05

BF16 = jnp.bfloat16
F32 = jnp.float32

SEQ = ("y_lo", "z")
CHAN = ("x", "y_hi", "core")
LINE = ("x", "core")
PLANE = ("y_lo", "z", "y_hi")
VMEM_LIMIT = 24 << 20


def split_halves(table):
    high = table.astype(jnp.bfloat16)
    low = (table - high.astype(np.float64)).astype(jnp.bfloat16)
    return [high, low]


def make_table(blocks, block, rows):
    length = blocks * block
    steps = np.arange(blocks)
    outer = np.exp(-2j * np.pi * np.outer(steps + 0.25, steps) / blocks)
    eye = np.eye(rows)
    first = np.kron(np.concatenate([outer.real, outer.imag], axis=0), eye)
    last = [np.kron(part.T, eye) / length for part in (outer.real, outer.imag)]
    twist = np.exp(-2j * np.pi * np.outer(steps + 0.25, np.arange(block)) / length)
    twist = np.repeat(np.concatenate([twist.real, twist.imag], axis=1), rows, axis=0)
    angle = 2 * np.pi * (np.outer(np.arange(block), np.arange(block)) % block) / block
    inner = np.block([[np.cos(angle), -np.sin(angle)], [np.sin(angle), np.cos(angle)]])
    parts = split_halves(first) + split_halves(inner) + split_halves(twist)
    parts = parts + split_halves(last[0]) + split_halves(last[1])
    return np.concatenate(parts, axis=0)


class Table:
    def __init__(self, ref):
        self.ref = ref
        self.size = ref.shape[1]
        self.block = self.size // 2
        size = self.size
        self.first = [(0, 2 * size), (2 * size, 2 * size)]
        self.inner = [(4 * size, size), (5 * size, size)]
        self.twist = [(6 * size, size), (7 * size, size)]
        self.last = [[(8 * size, size), (9 * size, size)], [(10 * size, size), (11 * size, size)]]

    def rows(self, span):
        return self.ref[span[0] : span[0] + span[1], :]

    def turns(self):
        wide = self.rows(self.twist[0]).astype(F32) + self.rows(self.twist[1]).astype(F32)
        return (wide[:, : self.block], wide[:, self.block :])


def halves(wide):
    high = wide.astype(BF16)
    low = (wide - high.astype(F32)).astype(BF16)
    return (high, low)


def mul(left, right, flip=False):
    dims = (((1,), (1 if flip else 0,)), ((), ()))
    return lax.dot_general(left, right, dims, preferred_element_type=F32)


def to_values(signal, table, turn_re, turn_im):
    rows, width = signal.shape
    block = table.block
    part = mul(table.rows(table.first[0]), signal) + mul(table.rows(table.first[1]), signal)
    turned = []
    for i in range(width // block):
        part_re = part[:rows, i * block : (i + 1) * block]
        part_im = part[rows:, i * block : (i + 1) * block]
        turned.append(
            jnp.concatenate(
                [part_re * turn_re - part_im * turn_im, part_re * turn_im + part_im * turn_re],
                axis=1,
            )
        )
    high, low = halves(jnp.concatenate(turned, axis=0))
    inner = [table.rows(span) for span in table.inner]
    values = mul(high, inner[0]) + (mul(high, inner[1]) + mul(low, inner[0]))
    return [
        (values[i * rows : (i + 1) * rows, :block], values[i * rows : (i + 1) * rows, block:])
        for i in range(width // block)
    ]


def to_signal(value_re, value_im, table, turn_re, turn_im):
    block = table.block
    high, low = halves(jnp.concatenate([value_re, value_im], axis=1))
    inner = [table.rows(span) for span in table.inner]
    back = mul(high, inner[0], True) + (mul(high, inner[1], True) + mul(low, inner[0], True))
    back_re, back_im = back[:, :block], back[:, block:]
    turned = (back_re * turn_re + back_im * turn_im, back_im * turn_re - back_re * turn_im)
    out = None
    for wide, (span_high, span_low) in zip(turned, table.last):
        high, low = halves(wide)
        last = table.rows(span_high)
        term = mul(last, high) + (mul(last, low) + mul(table.rows(span_low), high))
        out = term if out is None else out + term
    return out


def call(body, name, args, outs, scratch=()):
    whole = pl.BlockSpec(memory_space=pltpu.VMEM)
    apart = pl.BlockSpec(memory_space=pltpu.HBM)
    return pl.pallas_call(
        body,
        out_shape=[
            (pltpu.VMEM if keep else pltpu.HBM)(shape, dtype)
            for shape, dtype, keep in outs
        ],
        in_specs=[whole if keep else apart for _, keep in args],
        out_specs=[whole if keep else apart for _, _, keep in outs],
        scratch_shapes=list(scratch),
        compiler_params=pltpu.CompilerParams(vmem_limit_bytes=VMEM_LIMIT),
        name=name,
    )(
        *[
            pltpu.with_memory_space_constraint(x, pltpu.VMEM if keep else pltpu.HBM)
            for x, keep in args
        ]
    )


def source_body(
    key_hbm,
    value_hbm,
    filter_hbm,
    query_hbm,
    grad_hbm,
    gain_hbm,
    table_hbm,
    packed_ref,
    key_ref,
    value_ref,
    query_ref,
    grad_ref,
    gain_ref,
    table_ref,
    filter_ref,
    sems,
):
    pairs = [
        (query_hbm, query_ref),
        (grad_hbm, grad_ref),
        (key_hbm, key_ref),
        (value_hbm, value_ref),
        (filter_hbm, filter_ref),
        (gain_hbm, gain_ref),
        (table_hbm, table_ref),
    ]
    copies = [pltpu.make_async_copy(a, b, sems.at[i]) for i, (a, b) in enumerate(pairs)]
    for copy in copies:
        copy.start()
    peers, rows, block = packed_ref.shape
    per = rows // 4

    def piece(wide):
        return wide.reshape(peers, per, block)

    for copy in copies[:2]:
        copy.wait()
    query = piece(query_ref[...].astype(F32).T)
    grad = piece(grad_ref[...].astype(F32).T)
    packed_ref[:, 2 * per :, :] = jnp.concatenate([query, grad], axis=1).astype(BF16)
    for copy in copies[2:5]:
        copy.wait()
    source = (key_ref[...].astype(F32) * value_ref[...].astype(F32)).astype(BF16).astype(F32)
    taps = piece(filter_ref[...].astype(F32))
    packed_ref[:, : 2 * per, :] = jnp.concatenate([piece(source.T), taps], axis=1).astype(BF16)
    for copy in copies[5:]:
        copy.wait()


def convolve_body(packed_ref, gain_ref, table_ref, out_ref, values_ref, gained_ref, sums_ref):
    table = Table(table_ref)
    turns = table.turns()
    peers, rows, block = packed_ref.shape
    per = rows // 4
    packed = packed_ref[:, : 2 * per, :].astype(F32)
    source = packed[:, :per].reshape(peers * per, block)
    taps = packed[:, per:].reshape(peers * per, block)
    signal = jnp.concatenate([source, taps], axis=1).astype(BF16)
    (src_re, src_im), (tap_re, tap_im) = to_values(signal, table, *turns)
    values_ref[0] = tap_re
    values_ref[1] = tap_im
    others = packed_ref[:, 2 * per :, :].astype(F32)
    query, grad = others[:, :per], others[:, per:]
    wide = gain_ref.shape[1]
    lane = lax.broadcasted_iota(jnp.int32, (per, wide), 1)
    channel = lax.broadcasted_iota(jnp.int32, (per, wide), 0) + per * lax.axis_index(SEQ)
    picked = jnp.where(lane == channel, jnp.broadcast_to(gain_ref[...], (per, wide)), 0.0)
    gained = grad * jnp.sum(picked, axis=1, keepdims=True)[None]
    gained_ref[...] = gained
    out = to_signal(
        src_re * tap_re - src_im * tap_im, src_re * tap_im + src_im * tap_re, table, *turns
    )
    conv = out.reshape(peers, per, block).astype(BF16)
    out_ref[...] = conv
    product = (query * conv.astype(F32)).astype(BF16).astype(F32)
    square = jnp.sum(product * product, axis=1, keepdims=True)
    cross = jnp.sum(gained * product, axis=1, keepdims=True)
    half = peers // 2
    sums_ref[...] = jnp.concatenate(
        [square[:half], square[half:], cross[:half], cross[half:]], axis=1
    )


def merge_body(sums_ref, out_ref):
    total = jnp.sum(sums_ref[...].astype(F32), axis=0, keepdims=True)
    out_ref[...] = jnp.broadcast_to(total, out_ref.shape).astype(out_ref.dtype)


def scales_of(square, cross, width):
    scale = lax.rsqrt(square / width + EPSILON)
    return (scale, cross * scale * scale * scale / width)


def correlate_body(
    sums_ref, packed_ref, conv_ref, gained_ref, values_ref, table_ref, out_ref, *, width
):
    table = Table(table_ref)
    turns = table.turns()
    peers, per, block = conv_ref.shape
    square = jnp.concatenate([sums_ref[:, 0:1, :], sums_ref[:, 1:2, :]], axis=0)
    cross = jnp.concatenate([sums_ref[:, 2:3, :], sums_ref[:, 3:4, :]], axis=0)
    scale, pull = scales_of(square, cross, width)
    conv = conv_ref[...].astype(F32)
    query = packed_ref[:, 2 * per :, :].astype(F32)[:, :per]
    product = (query * conv).astype(BF16).astype(F32)
    grad = (gained_ref[...] * scale - product * pull).astype(BF16).astype(F32)
    signal = (grad * query).reshape(peers * per, block).astype(BF16)
    ((sig_re, sig_im),) = to_values(signal, table, *turns)
    tap_re, tap_im = values_ref[0], values_ref[1]
    out = to_signal(
        sig_re * tap_re + sig_im * tap_im, sig_im * tap_re - sig_re * tap_im, table, *turns
    )
    spread = out.reshape(peers, per, block)
    out_ref[...] = jnp.concatenate([conv, spread], axis=1).astype(BF16)


def finish_body(
    back_ref,
    sums_ref,
    key_ref,
    value_ref,
    query_ref,
    grad_ref,
    gain_ref,
    normed_hbm,
    query_grad_hbm,
    key_grad_hbm,
    value_grad_hbm,
    outs_ref,
    sems,
    *,
    width,
):
    peers, rows, block = back_ref.shape
    per = rows // 2
    outs = [normed_hbm, query_grad_hbm, key_grad_hbm, value_grad_hbm]
    copies = [pltpu.make_async_copy(outs_ref.at[i], out, sems.at[i]) for i, out in enumerate(outs)]

    def put(i, wide):
        outs_ref[i] = wide.astype(BF16)
        copies[i].start()

    back = back_ref[...].astype(F32)
    spread = back[:, per:].reshape(peers * per, block).T
    put(2, spread * value_ref[...].astype(F32))
    put(3, spread * key_ref[...].astype(F32))
    half = peers // 2
    place = lax.axis_index(SEQ)
    mine = sums_ref[place % half]
    upper = place >= half
    square = jnp.where(upper, mine[1:2], mine[0:1])
    cross = jnp.where(upper, mine[3:4], mine[2:3])
    scale, pull = scales_of(square, cross, width)
    tall = (block, block)
    scale = jnp.broadcast_to(scale, tall).T[:, 0:1]
    pull = jnp.broadcast_to(pull, tall).T[:, 0:1]
    conv = back[:, :per].reshape(peers * per, block).T
    gain = gain_ref[...]
    product = (query_ref[...].astype(F32) * conv).astype(BF16).astype(F32)
    put(0, product * scale * gain)
    gained = grad_ref[...].astype(F32) * gain
    grad = (gained * scale - product * pull).astype(BF16).astype(F32)
    put(1, grad * conv)
    for copy in copies:
        copy.wait()


def per_device(query, key, value, filters, gain, out_grad):
    peers = lax.axis_size(SEQ)
    groups = lax.axis_size(CHAN)
    line = lax.axis_size(LINE)
    plane = lax.axis_size(PLANE)
    block, wide = query.shape
    per = wide // peers
    width = float(wide * groups)
    table = jnp.asarray(make_table(peers, block, per))
    gain = gain.reshape(1, wide)
    home = (block, wide)
    owned = (peers, per, block)
    chunk = 2 * peers // line

    def exchange(array, axes):
        return lax.all_to_all(array, axes, split_axis=0, concat_axis=0, tiled=True)

    def merge(array, count, dtype, name):
        return call(
            merge_body, name, [(array, True)], [((count, chunk, block), dtype, True)]
        )[0]

    def dma(count):
        return pltpu.SemaphoreType.DMA((count,))

    packed, key, value, query, out_grad, gain, table = call(
        source_body,
        "source",
        [(x, False) for x in (key, value, filters, query, out_grad, gain, table)],
        [((peers, 4 * per, block), BF16, True)]
        + [(home, BF16, True)] * 4
        + [((1, wide), F32, True), (table.shape, BF16, True)],
        [pltpu.VMEM((wide, block), BF16), dma(7)],
    )
    packed = exchange(packed, SEQ)
    conv, values, gained, sums = call(
        convolve_body,
        "convolve",
        [(x, True) for x in (packed, gain, table)],
        [
            (owned, BF16, True),
            ((2, wide, block), F32, True),
            (owned, F32, True),
            ((line, chunk, block), F32, True),
        ],
    )
    sums = exchange(sums, LINE)
    sums = exchange(merge(sums, plane, F32, "merge_line"), PLANE)
    sums = exchange(merge(sums, line, F32, "merge_plane"), LINE)
    (back,) = call(
        functools.partial(correlate_body, width=width),
        "correlate",
        [(x, True) for x in (sums, packed, conv, gained, values, table)],
        [((peers, 2 * per, block), BF16, True)],
    )
    back = exchange(back, SEQ)
    return tuple(
        call(
            functools.partial(finish_body, width=width),
            "finish",
            [(x, True) for x in (back, sums, key, value, query, out_grad, gain)],
            [(home, BF16, False)] * 4,
            [pltpu.VMEM((4,) + home, BF16), dma(4)],
        )
    )


def solution(mesh):
    cut = jax.sharding.Mesh(mesh.devices.reshape(4, 8, 8, 2, 2), SEQ + CHAN)
    tokens = P(SEQ, CHAN)
    return jax.shard_map(
        per_device,
        mesh=cut,
        in_specs=(tokens, tokens, tokens, P(CHAN, SEQ), P(CHAN), tokens),
        out_specs=(tokens, tokens, tokens, tokens),
        check_vma=False,
    )
```

time: 99 us -> 96.6 us (0.976)
  blocking collectives: 91.7 us -> 90 us
    all_to_all x5, blocking collectives: 91.7 us -> 90 us  [exchange(): return lax.all_to_all(array, axes, split_axis=0, concat_axis=0, tiled=True)]
where the time goes in v3:
time: 96.6 us; the launch traced here: 96.3 us
  blocking collectives  90 us (93%)
  Pallas kernels  5.64 us (6%)
    all_to_all x5, blocking collectives, exchange(): return lax.all_to_all(array, axes, split_axis=0, concat_axis=0, tiled=True)  90 us
    pallas_call x6, Pallas kernels, call(): pl.pallas_call(body, out_shape=[(pltpu.VMEM if keep else pltpu.HBM)(shape...  5.64 us

profile of v3, /device:TPU:1, one launch (start us, length us, event | category | flops | bytes accessed | tf_op | source)
XLA Modules:
  0.0 96.3 jit_solution(464673033673386201)
XLA Ops:
  0.6 1.7 %source.1 = (bf16[32,32,128]{2,1,0:T(8,128)(2,1)S(1)}, bf16[128,256]{1,0:T(8,128)(2,1)S(1)}, bf16[128,256]{1,0:T(8,128)(2,1)S(1)}, bf16[128,256]{1,0:T(8,128)(2,...) custom-call(bf16[128,256]{1,0:T(8,128)(2,1)} %key_hbm.1, ...), custom_call_target="tpu_custom_call" | custom-call | tf_op jit(solution)/shard_map/source/pallas_call | solution.py:118
  2.3 31.7 %all_to_all.25.packed_ref = bf16[32,32,128]{2,1,0:T(8,128)(2,1)S(1)} all-to-all(bf16[32,32,128]{2,1,0:T(8,128)(2,1)S(1)} %get-tuple-element.15), channel_id=1, replica_groups=mesh['y_lo'=4,'z'=8,'x'=8,'y_hi'=2,'core'=2] {'y_lo','z'}, dimensions={0} | all-to-all | bytes 524288 | tf_op jit(solution)/shard_map/all_to_all | solution.py:320
  34.0 1.5 %convolve.1 = (bf16[32,8,128]{2,1,0:T(8,128)(2,1)S(1)}, f32[2,256,128]{2,1,0:T(8,128)S(1)}, f32[32,8,128]{2,1,0:T(8,128)S(1)}, f32[16,4,128]{2,1,0:T(4,128)S(1)}) custom-call(bf16[32,32,128]{2,1,0:T(8,128)(2,1)S(1)} %all_to_all.25.packed_ref, f32[1,256]{1,0:T(1,128)S(1)} %get-tuple-element.16.gain_ref, bf16[3072,256]{1,0:T(8,128)(2,1)S(1)} %get-tuple-element.17.table_ref), custom_call_target="tpu_custom_call" | custom-call | tf_op jit(solution)/shard_map/convolve/pallas_call | solution.py:118
  35.6 16.0 %all_to_all.26.sums_ref = f32[16,4,128]{2,1,0:T(4,128)S(1)} all-to-all(f32[16,4,128]{2,1,0:T(4,128)S(1)} %get-tuple-element.18), channel_id=1, replica_groups=mesh['y_lo'=4,'z'=8,'x'=8,'y_hi'=2,'core'=2] {'x','core'}, dimensions={0} | all-to-all | bytes 65536 | tf_op jit(solution)/shard_map/all_to_all | solution.py:320
  51.6 18.2 %all_to_all.27.sums_ref = f32[64,4,128]{2,1,0:T(4,128)S(1)} all-to-all(f32[64,4,128]{2,1,0:T(4,128)S(1)} %merge_line.1), channel_id=1, replica_groups=mesh['y_lo'=4,'z'=8,'x'=8,'y_hi'=2,'core'=2] {'y_lo','z','y_hi'}, dimensions={0} | all-to-all | bytes 262144 | tf_op jit(solution)/shard_map/all_to_all | solution.py:320
  69.8 0.1 merge_plane.1
  69.8 11.8 %all_to_all.28.sums_ref = f32[16,4,128]{2,1,0:T(4,128)S(1)} all-to-all(f32[16,4,128]{2,1,0:T(4,128)S(1)} %merge_plane.1), channel_id=1, replica_groups=mesh['y_lo'=4,'z'=8,'x'=8,'y_hi'=2,'core'=2] {'x','core'}, dimensions={0} | all-to-all | bytes 65536 | tf_op jit(solution)/shard_map/all_to_all | solution.py:320
  81.6 1.4 %correlate.1 = bf16[32,16,128]{2,1,0:T(8,128)(2,1)S(1)} custom-call(f32[16,4,128]{2,1,0:T(4,128)S(1)} %all_to_all.28.sums_ref, bf16[32,32,128]{2,1,0:T(8,128)(2,1)S(1)} %all_to_all.25.packed_ref, bf16[32,8,128]{2,1,0:T(8,128)(2,1)S(1)} %get-tuple-element.19.conv_ref, f32[32,8,128]{2,1,0:T(8,128)S(1)} %get-tuple-element.20.gained_ref, ...), custom_call_target="tpu_custom_call" | custom-call | tf_op jit(solution)/shard_map/correlate/pallas_call | solution.py:118
  83.0 12.3 %all_to_all.29.back_ref = bf16[32,16,128]{2,1,0:T(8,128)(2,1)S(1)} all-to-all(bf16[32,16,128]{2,1,0:T(8,128)(2,1)S(1)} %correlate.1), channel_id=1, replica_groups=mesh['y_lo'=4,'z'=8,'x'=8,'y_hi'=2,'core'=2] {'y_lo','z'}, dimensions={0} | all-to-all | bytes 262144 | tf_op jit(solution)/shard_map/all_to_all | solution.py:320
  95.4 0.9 finish.1
  (1 shorter events, 0.0 us)

commit v4 on v3

--- a/solution.py
+++ b/solution.py
@@ -27,7 +27,7 @@
     return [high, low]
 
 
-def make_table(blocks, block, rows):
+def make_tables(blocks, block, rows):
     length = blocks * block
     steps = np.arange(blocks)
     outer = np.exp(-2j * np.pi * np.outer(steps + 0.25, steps) / blocks)
@@ -35,31 +35,29 @@
     first = np.kron(np.concatenate([outer.real, outer.imag], axis=0), eye)
     last = [np.kron(part.T, eye) / length for part in (outer.real, outer.imag)]
     twist = np.exp(-2j * np.pi * np.outer(steps + 0.25, np.arange(block)) / length)
-    twist = np.repeat(np.concatenate([twist.real, twist.imag], axis=1), rows, axis=0)
+    twist = np.concatenate([twist.real, twist.imag], axis=1).astype(np.float32)
     angle = 2 * np.pi * (np.outer(np.arange(block), np.arange(block)) % block) / block
     inner = np.block([[np.cos(angle), -np.sin(angle)], [np.sin(angle), np.cos(angle)]])
-    parts = split_halves(first) + split_halves(inner) + split_halves(twist)
+    parts = split_halves(first) + split_halves(inner)
     parts = parts + split_halves(last[0]) + split_halves(last[1])
-    return np.concatenate(parts, axis=0)
+    return (np.concatenate(parts, axis=0), twist)
 
 
 class Table:
-    def __init__(self, ref):
+    def __init__(self, ref, twist_ref):
         self.ref = ref
-        self.size = ref.shape[1]
-        self.block = self.size // 2
-        size = self.size
+        self.size = size = ref.shape[1]
+        self.block = size // 2
         self.first = [(0, 2 * size), (2 * size, 2 * size)]
         self.inner = [(4 * size, size), (5 * size, size)]
-        self.twist = [(6 * size, size), (7 * size, size)]
-        self.last = [[(8 * size, size), (9 * size, size)], [(10 * size, size), (11 * size, size)]]
+        self.last = [[(6 * size, size), (7 * size, size)], [(8 * size, size), (9 * size, size)]]
+        peers = twist_ref.shape[0]
+        tall = (peers, size // peers, size)
+        twist = jnp.broadcast_to(twist_ref[...].reshape(peers, 1, size), tall).reshape(size, size)
+        self.turns = (twist[:, : self.block], twist[:, self.block :])
 
     def rows(self, span):
         return self.ref[span[0] : span[0] + span[1], :]
-
-    def turns(self):
-        wide = self.rows(self.twist[0]).astype(F32) + self.rows(self.twist[1]).astype(F32)
-        return (wide[:, : self.block], wide[:, self.block :])
 
 
 def halves(wide):
@@ -106,8 +104,8 @@
     out = None
     for wide, (span_high, span_low) in zip(turned, table.last):
         high, low = halves(wide)
-        last = table.rows(span_high)
-        term = mul(last, high) + (mul(last, low) + mul(table.rows(span_low), high))
+        both = mul(table.rows(span_high), jnp.concatenate([high, low], axis=1))
+        term = both[:, :block] + (both[:, block:] + mul(table.rows(span_low), high))
         out = term if out is None else out + term
     return out
 
@@ -142,6 +140,7 @@
     grad_hbm,
     gain_hbm,
     table_hbm,
+    twist_hbm,
     packed_ref,
     key_ref,
     value_ref,
@@ -149,6 +148,7 @@
     grad_ref,
     gain_ref,
     table_ref,
+    twist_ref,
     filter_ref,
     sems,
 ):
@@ -159,10 +159,12 @@
         (value_hbm, value_ref),
         (filter_hbm, filter_ref),
         (gain_hbm, gain_ref),
+        (twist_hbm, twist_ref),
         (table_hbm, table_ref),
     ]
     copies = [pltpu.make_async_copy(a, b, sems.at[i]) for i, (a, b) in enumerate(pairs)]
-    for copy in copies:
+    copies[-1].start()
+    for copy in copies[:-1]:
         copy.start()
     peers, rows, block = packed_ref.shape
     per = rows // 4
@@ -184,9 +186,11 @@
         copy.wait()
 
 
-def convolve_body(packed_ref, gain_ref, table_ref, out_ref, values_ref, gained_ref, sums_ref):
-    table = Table(table_ref)
-    turns = table.turns()
+def convolve_body(
+    packed_ref, gain_ref, table_ref, twist_ref, out_ref, values_ref, gained_ref, sums_ref
+):
+    table = Table(table_ref, twist_ref)
+    turns = table.turns
     peers, rows, block = packed_ref.shape
     per = rows // 4
     packed = packed_ref[:, : 2 * per, :].astype(F32)
@@ -229,10 +233,19 @@
 
 
 def correlate_body(
-    sums_ref, packed_ref, conv_ref, gained_ref, values_ref, table_ref, out_ref, *, width
+    sums_ref,
+    packed_ref,
+    conv_ref,
+    gained_ref,
+    values_ref,
+    table_ref,
+    twist_ref,
+    out_ref,
+    *,
+    width,
 ):
-    table = Table(table_ref)
-    turns = table.turns()
+    table = Table(table_ref, twist_ref)
+    turns = table.turns
     peers, per, block = conv_ref.shape
     square = jnp.concatenate([sums_ref[:, 0:1, :], sums_ref[:, 1:2, :]], axis=0)
     cross = jnp.concatenate([sums_ref[:, 2:3, :], sums_ref[:, 3:4, :]], axis=0)
@@ -310,7 +323,7 @@
     block, wide = query.shape
     per = wide // peers
     width = float(wide * groups)
-    table = jnp.asarray(make_table(peers, block, per))
+    table, twist = (jnp.asarray(part) for part in make_tables(peers, block, per))
     gain = gain.reshape(1, wide)
     home = (block, wide)
     owned = (peers, per, block)
@@ -327,20 +340,20 @@
     def dma(count):
         return pltpu.SemaphoreType.DMA((count,))
 
-    packed, key, value, query, out_grad, gain, table = call(
+    packed, key, value, query, out_grad, gain, table, twist = call(
         source_body,
         "source",
-        [(x, False) for x in (key, value, filters, query, out_grad, gain, table)],
+        [(x, False) for x in (key, value, filters, query, out_grad, gain, table, twist)],
         [((peers, 4 * per, block), BF16, True)]
         + [(home, BF16, True)] * 4
-        + [((1, wide), F32, True), (table.shape, BF16, True)],
-        [pltpu.VMEM((wide, block), BF16), dma(7)],
+        + [((1, wide), F32, True), (table.shape, BF16, True), (twist.shape, F32, True)],
+        [pltpu.VMEM((wide, block), BF16), dma(8)],
     )
     packed = exchange(packed, SEQ)
     conv, values, gained, sums = call(
         convolve_body,
         "convolve",
-        [(x, True) for x in (packed, gain, table)],
+        [(x, True) for x in (packed, gain, table, twist)],
         [
             (owned, BF16, True),
             ((2, wide, block), F32, True),
@@ -349,12 +362,12 @@
         ],
     )
     sums = exchange(sums, LINE)
-    sums = exchange(merge(sums, plane, F32, "merge_line"), PLANE)
+    sums = exchange(merge(sums, plane, BF16, "merge_line"), PLANE)
     sums = exchange(merge(sums, line, F32, "merge_plane"), LINE)
     (back,) = call(
         functools.partial(correlate_body, width=width),
         "correlate",
-        [(x, True) for x in (sums, packed, conv, gained, values, table)],
+        [(x, True) for x in (sums, packed, conv, gained, values, table, twist)],
         [((peers, 2 * per, block), BF16, True)],
     )
     back = exchange(back, SEQ)

time: 96.6 us -> 95.7 us (level)
  no operation moved by 1% of the time
where the time goes in v4:
time: 95.7 us; the launch traced here: 95.4 us
  blocking collectives  89.4 us (93%)
  Pallas kernels  5.38 us (6%)
    all_to_all x5, blocking collectives, exchange(): return lax.all_to_all(array, axes, split_axis=0, concat_axis=0, tiled=True)  89.4 us
    pallas_call x6, Pallas kernels, call(): pl.pallas_call(body, out_shape=[(pltpu.VMEM if keep else pltpu.HBM)(shape...  5.38 us

profile of v4, /device:TPU:1, one launch (start us, length us, event | category | flops | bytes accessed | tf_op | source)
XLA Modules:
  0.0 95.4 jit_solution(10856482858780532135)
XLA Ops:
  0.6 1.5 %source.1 = (bf16[32,32,128]{2,1,0:T(8,128)(2,1)S(1)}, bf16[128,256]{1,0:T(8,128)(2,1)S(1)}, bf16[128,256]{1,0:T(8,128)(2,1)S(1)}, bf16[128,256]{1,0:T(8,128)(2,...) custom-call(bf16[128,256]{1,0:T(8,128)(2,1)} %key_hbm.1, ...), custom_call_target="tpu_custom_call" | custom-call | tf_op jit(solution)/shard_map/source/pallas_call | solution.py:116
  2.2 31.7 %all_to_all.25.packed_ref = bf16[32,32,128]{2,1,0:T(8,128)(2,1)S(1)} all-to-all(bf16[32,32,128]{2,1,0:T(8,128)(2,1)S(1)} %get-tuple-element.16), channel_id=1, replica_groups=mesh['y_lo'=4,'z'=8,'x'=8,'y_hi'=2,'core'=2] {'y_lo','z'}, dimensions={0} | all-to-all | bytes 524288 | tf_op jit(solution)/shard_map/all_to_all | solution.py:333
  33.9 1.5 %convolve.1 = (bf16[32,8,128]{2,1,0:T(8,128)(2,1)S(1)}, f32[2,256,128]{2,1,0:T(8,128)S(1)}, f32[32,8,128]{2,1,0:T(8,128)S(1)}, f32[16,4,128]{2,1,0:T(4,128)S(1)}) custom-call(bf16[32,32,128]{2,1,0:T(8,128)(2,1)S(1)} %all_to_all.25.packed_ref, f32[1,256]{1,0:T(1,128)S(1)} %get-tuple-element.17.gain_ref, bf16[2560,256]{1,0:T(8,128)(2,1)S(1)} %get-tuple-element.18.table_ref, ...), custom_call_target="tpu_custom_call" | custom-call | tf_op jit(solution)/shard_map/convolve/pallas_call | solution.py:116
  35.4 16.0 %all_to_all.26.sums_ref = f32[16,4,128]{2,1,0:T(4,128)S(1)} all-to-all(f32[16,4,128]{2,1,0:T(4,128)S(1)} %get-tuple-element.20), channel_id=1, replica_groups=mesh['y_lo'=4,'z'=8,'x'=8,'y_hi'=2,'core'=2] {'x','core'}, dimensions={0} | all-to-all | bytes 65536 | tf_op jit(solution)/shard_map/all_to_all | solution.py:333
  51.4 17.8 %all_to_all.27.sums_ref = bf16[64,4,128]{2,1,0:T(4,128)(2,1)S(1)} all-to-all(bf16[64,4,128]{2,1,0:T(4,128)(2,1)S(1)} %merge_line.1), channel_id=1, replica_groups=mesh['y_lo'=4,'z'=8,'x'=8,'y_hi'=2,'core'=2] {'y_lo','z','y_hi'}, dimensions={0} | all-to-all | bytes 131072 | tf_op jit(solution)/shard_map/all_to_all | solution.py:333
  69.1 0.1 merge_plane.1
  69.2 11.6 %all_to_all.28.sums_ref = f32[16,4,128]{2,1,0:T(4,128)S(1)} all-to-all(f32[16,4,128]{2,1,0:T(4,128)S(1)} %merge_plane.1), channel_id=1, replica_groups=mesh['y_lo'=4,'z'=8,'x'=8,'y_hi'=2,'core'=2] {'x','core'}, dimensions={0} | all-to-all | bytes 65536 | tf_op jit(solution)/shard_map/all_to_all | solution.py:333
  80.8 1.3 %correlate.1 = bf16[32,16,128]{2,1,0:T(8,128)(2,1)S(1)} custom-call(f32[16,4,128]{2,1,0:T(4,128)S(1)} %all_to_all.28.sums_ref, bf16[32,32,128]{2,1,0:T(8,128)(2,1)S(1)} %all_to_all.25.packed_ref, bf16[32,8,128]{2,1,0:T(8,128)(2,1)S(1)} %get-tuple-element.21.conv_ref, f32[32,8,128]{2,1,0:T(8,128)S(1)} %get-tuple-element.22.gained_ref, ...), custom_call_target="tpu_custom_call" | custom-call | tf_op jit(solution)/shard_map/correlate/pallas_call | solution.py:116
  82.2 12.3 %all_to_all.29.back_ref = bf16[32,16,128]{2,1,0:T(8,128)(2,1)S(1)} all-to-all(bf16[32,16,128]{2,1,0:T(8,128)(2,1)S(1)} %correlate.1), channel_id=1, replica_groups=mesh['y_lo'=4,'z'=8,'x'=8,'y_hi'=2,'core'=2] {'y_lo','z'}, dimensions={0} | all-to-all | bytes 262144 | tf_op jit(solution)/shard_map/all_to_all | solution.py:333
  94.5 0.9 finish.1
  (1 shorter events, 0.0 us)

commit v5 on v4

--- a/solution.py
+++ b/solution.py
@@ -110,7 +110,7 @@
     return out
 
 
-def call(body, name, args, outs, scratch=()):
+def call(body, name, args, outs, scratch=(), cost=None):
     whole = pl.BlockSpec(memory_space=pltpu.VMEM)
     apart = pl.BlockSpec(memory_space=pltpu.HBM)
     return pl.pallas_call(
@@ -122,6 +122,7 @@
         in_specs=[whole if keep else apart for _, keep in args],
         out_specs=[whole if keep else apart for _, _, keep in outs],
         scratch_shapes=list(scratch),
+        cost_estimate=cost,
         compiler_params=pltpu.CompilerParams(vmem_limit_bytes=VMEM_LIMIT),
         name=name,
     )(
@@ -132,58 +133,31 @@
     )
 
 
-def source_body(
-    key_hbm,
-    value_hbm,
-    filter_hbm,
-    query_hbm,
-    grad_hbm,
-    gain_hbm,
-    table_hbm,
-    twist_hbm,
-    packed_ref,
-    key_ref,
-    value_ref,
-    query_ref,
-    grad_ref,
-    gain_ref,
-    table_ref,
-    twist_ref,
-    filter_ref,
-    sems,
-):
-    pairs = [
-        (query_hbm, query_ref),
-        (grad_hbm, grad_ref),
-        (key_hbm, key_ref),
-        (value_hbm, value_ref),
-        (filter_hbm, filter_ref),
-        (gain_hbm, gain_ref),
-        (twist_hbm, twist_ref),
-        (table_hbm, table_ref),
+def load_body(*refs):
+    count = len(refs) // 2
+    sems = refs[-1]
+    copies = [
+        pltpu.make_async_copy(refs[i], refs[count + i], sems.at[i]) for i in range(count)
     ]
-    copies = [pltpu.make_async_copy(a, b, sems.at[i]) for i, (a, b) in enumerate(pairs)]
-    copies[-1].start()
-    for copy in copies[:-1]:
+    for copy in copies:
         copy.start()
+    for copy in copies:
+        copy.wait()
+
+
+def pack_body(key_ref, value_ref, filter_ref, query_ref, grad_ref, packed_ref):
     peers, rows, block = packed_ref.shape
     per = rows // 4
 
     def piece(wide):
         return wide.reshape(peers, per, block)
 
-    for copy in copies[:2]:
-        copy.wait()
     query = piece(query_ref[...].astype(F32).T)
     grad = piece(grad_ref[...].astype(F32).T)
     packed_ref[:, 2 * per :, :] = jnp.concatenate([query, grad], axis=1).astype(BF16)
-    for copy in copies[2:5]:
-        copy.wait()
     source = (key_ref[...].astype(F32) * value_ref[...].astype(F32)).astype(BF16).astype(F32)
     taps = piece(filter_ref[...].astype(F32))
     packed_ref[:, : 2 * per, :] = jnp.concatenate([piece(source.T), taps], axis=1).astype(BF16)
-    for copy in copies[5:]:
-        copy.wait()
 
 
 def convolve_body(
@@ -340,14 +314,20 @@
     def dma(count):
         return pltpu.SemaphoreType.DMA((count,))
 
-    packed, key, value, query, out_grad, gain, table, twist = call(
-        source_body,
-        "source",
-        [(x, False) for x in (key, value, filters, query, out_grad, gain, table, twist)],
-        [((peers, 4 * per, block), BF16, True)]
-        + [(home, BF16, True)] * 4
-        + [((1, wide), F32, True), (table.shape, BF16, True), (twist.shape, F32, True)],
-        [pltpu.VMEM((wide, block), BF16), dma(8)],
+    loads = [key, value, filters, query, out_grad, gain, twist]
+    key, value, filters, query, out_grad, gain, twist = call(
+        load_body,
+        "load",
+        [(x, False) for x in loads],
+        [(x.shape, x.dtype, True) for x in loads],
+        [dma(len(loads))],
+    )
+    (packed,) = call(
+        pack_body,
+        "pack",
+        [(x, True) for x in (key, value, filters, query, out_grad)],
+        [((peers, 4 * per, block), BF16, True)],
+        cost=pl.CostEstimate(flops=10**11, bytes_accessed=10**7, transcendentals=0),
     )
     packed = exchange(packed, SEQ)
     conv, values, gained, sums = call(

time: 95.7 us -> 95.5 us (level)
    pallas_call x6 -> x7, Pallas kernels: 5.38 us -> 5 us  [call(): pl.pallas_call(body, out_shape=[(pltpu.VMEM if keep else pltpu.HBM)(shape...]
where the time goes in v5:
time: 95.5 us; the launch traced here: 95.2 us
  blocking collectives  89.5 us (94%)
  Pallas kernels  5 us (5%)
    all_to_all x5, blocking collectives, exchange(): return lax.all_to_all(array, axes, split_axis=0, concat_axis=0, tiled=True)  89.5 us
    pallas_call x7, Pallas kernels, call(): pl.pallas_call(body, out_shape=[(pltpu.VMEM if keep else pltpu.HBM)(shape...  5 us

profile of v5, /device:TPU:1, one launch (start us, length us, event | category | flops | bytes accessed | tf_op | source)
XLA Modules:
  0.0 95.2 jit_solution(3616771629421499538)
XLA Ops:
  0.6 1.0 %load.1 = (bf16[128,256]{1,0:T(8,128)(2,1)S(1)}, bf16[128,256]{1,0:T(8,128)(2,1)S(1)}, bf16[256,128]{1,0:T(8,128)(2,1)S(1)}, bf16[128,256]{1,0:T(8,128)(2,1)S(1)...) custom-call(bf16[128,256]{1,0:T(8,128)(2,1)} %refs_0_.1, bf16[128,256]{1,0:T(8,128)(2,1)} %refs_1_.1, ...), custom_call_target="tpu_custom_call" | custom-call | tf_op jit(solution)/shard_map/load/pallas_call | solution.py:116
  1.7 0.0 copy-start
  1.7 0.1 pack.1
  1.8 31.8 %all_to_all.25.packed_ref = bf16[32,32,128]{2,1,0:T(8,128)(2,1)S(1)} all-to-all(bf16[32,32,128]{2,1,0:T(8,128)(2,1)S(1)} %pack.1), channel_id=1, replica_groups=mesh['y_lo'=4,'z'=8,'x'=8,'y_hi'=2,'core'=2] {'y_lo','z'}, dimensions={0} | all-to-all | bytes 524288 | tf_op jit(solution)/shard_map/all_to_all | solution.py:307
  33.7 0.0 copy-done
  33.7 1.5 %convolve.1 = (bf16[32,8,128]{2,1,0:T(8,128)(2,1)S(1)}, f32[2,256,128]{2,1,0:T(8,128)S(1)}, f32[32,8,128]{2,1,0:T(8,128)S(1)}, f32[16,4,128]{2,1,0:T(4,128)S(1)}) custom-call(bf16[32,32,128]{2,1,0:T(8,128)(2,1)S(1)} %all_to_all.25.packed_ref, f32[1,256]{1,0:T(1,128)S(1)} %get-tuple-element.20.gain_ref, bf16[2560,256]{1,0:T(8,128)(2,1)S(1)} %copy-done, ...), custom_call_target="tpu_custom_call" | custom-call | tf_op jit(solution)/shard_map/convolve/pallas_call | solution.py:116
  35.1 16.0 %all_to_all.26.sums_ref = f32[16,4,128]{2,1,0:T(4,128)S(1)} all-to-all(f32[16,4,128]{2,1,0:T(4,128)S(1)} %get-tuple-element.22), channel_id=1, replica_groups=mesh['y_lo'=4,'z'=8,'x'=8,'y_hi'=2,'core'=2] {'x','core'}, dimensions={0} | all-to-all | bytes 65536 | tf_op jit(solution)/shard_map/all_to_all | solution.py:307
  51.1 17.8 %all_to_all.27.sums_ref = bf16[64,4,128]{2,1,0:T(4,128)(2,1)S(1)} all-to-all(bf16[64,4,128]{2,1,0:T(4,128)(2,1)S(1)} %merge_line.1), channel_id=1, replica_groups=mesh['y_lo'=4,'z'=8,'x'=8,'y_hi'=2,'core'=2] {'y_lo','z','y_hi'}, dimensions={0} | all-to-all | bytes 131072 | tf_op jit(solution)/shard_map/all_to_all | solution.py:307
  68.9 0.1 merge_plane.1
  69.0 11.6 %all_to_all.28.sums_ref = f32[16,4,128]{2,1,0:T(4,128)S(1)} all-to-all(f32[16,4,128]{2,1,0:T(4,128)S(1)} %merge_plane.1), channel_id=1, replica_groups=mesh['y_lo'=4,'z'=8,'x'=8,'y_hi'=2,'core'=2] {'x','core'}, dimensions={0} | all-to-all | bytes 65536 | tf_op jit(solution)/shard_map/all_to_all | solution.py:307
  80.6 1.3 %correlate.1 = bf16[32,16,128]{2,1,0:T(8,128)(2,1)S(1)} custom-call(f32[16,4,128]{2,1,0:T(4,128)S(1)} %all_to_all.28.sums_ref, bf16[32,32,128]{2,1,0:T(8,128)(2,1)S(1)} %all_to_all.25.packed_ref, bf16[32,8,128]{2,1,0:T(8,128)(2,1)S(1)} %get-tuple-element.23.conv_ref, f32[32,8,128]{2,1,0:T(8,128)S(1)} %get-tuple-element.24.gained_ref, ...), custom_call_target="tpu_custom_call" | custom-call | tf_op jit(solution)/shard_map/correlate/pallas_call | solution.py:116
  82.0 12.3 %all_to_all.29.back_ref = bf16[32,16,128]{2,1,0:T(8,128)(2,1)S(1)} all-to-all(bf16[32,16,128]{2,1,0:T(8,128)(2,1)S(1)} %correlate.1), channel_id=1, replica_groups=mesh['y_lo'=4,'z'=8,'x'=8,'y_hi'=2,'core'=2] {'y_lo','z'}, dimensions={0} | all-to-all | bytes 262144 | tf_op jit(solution)/shard_map/all_to_all | solution.py:307
  94.3 0.9 finish.1
  (1 shorter events, 0.0 us)
Async XLA Ops:
  1.7 32.0 %copy-start = (bf16[2560,256]{1,0:T(8,128)(2,1)S(1)}, bf16[2560,256]{1,0:T(8,128)(2,1)}, u32[]{:S(2)}) copy-start(bf16[2560,256]{1,0:T(8,128)(2,1)} %constant.4.clone.table_ref) | copy-start | bytes 3932164

commit v6 on v5

--- a/solution.py
+++ b/solution.py
@@ -16,8 +16,8 @@
 
 SEQ = ("y_lo", "z")
 CHAN = ("x", "y_hi", "core")
-LINE = ("x", "core")
-PLANE = ("y_lo", "z", "y_hi")
+LINE = ("y_lo", "y_hi", "core")
+PLANE = ("x", "z")
 VMEM_LIMIT = 24 << 20
 
 

time: 95.5 us -> 95.7 us (level)
  no operation moved by 1% of the time
where the time goes in v6:
time: 95.7 us; the launch traced here: 95.3 us
  blocking collectives  89.6 us (94%)
  Pallas kernels  5 us (5%)
    all_to_all x5, blocking collectives, exchange(): return lax.all_to_all(array, axes, split_axis=0, concat_axis=0, tiled=True)  89.6 us
    pallas_call x7, Pallas kernels, call(): pl.pallas_call(body, out_shape=[(pltpu.VMEM if keep else pltpu.HBM)(shape...  5 us

profile of v6, /device:TPU:1, one launch (start us, length us, event | category | flops | bytes accessed | tf_op | source)
XLA Modules:
  0.0 95.3 jit_solution(4344267487648106274)
XLA Ops:
  0.6 1.0 %load.1 = (bf16[128,256]{1,0:T(8,128)(2,1)S(1)}, bf16[128,256]{1,0:T(8,128)(2,1)S(1)}, bf16[256,128]{1,0:T(8,128)(2,1)S(1)}, bf16[128,256]{1,0:T(8,128)(2,1)S(1)...) custom-call(bf16[128,256]{1,0:T(8,128)(2,1)} %refs_0_.1, bf16[128,256]{1,0:T(8,128)(2,1)} %refs_1_.1, ...), custom_call_target="tpu_custom_call" | custom-call | tf_op jit(solution)/shard_map/load/pallas_call | solution.py:116
  1.7 0.0 copy-start
  1.7 0.1 pack.1
  1.8 31.8 %all_to_all.25.packed_ref = bf16[32,32,128]{2,1,0:T(8,128)(2,1)S(1)} all-to-all(bf16[32,32,128]{2,1,0:T(8,128)(2,1)S(1)} %pack.1), channel_id=1, replica_groups=mesh['y_lo'=4,'z'=8,'x'=8,'y_hi'=2,'core'=2] {'y_lo','z'}, dimensions={0} | all-to-all | bytes 524288 | tf_op jit(solution)/shard_map/all_to_all | solution.py:307
  33.7 0.0 copy-done
  33.7 1.5 %convolve.1 = (bf16[32,8,128]{2,1,0:T(8,128)(2,1)S(1)}, f32[2,256,128]{2,1,0:T(8,128)S(1)}, f32[32,8,128]{2,1,0:T(8,128)S(1)}, f32[16,4,128]{2,1,0:T(4,128)S(1)}) custom-call(bf16[32,32,128]{2,1,0:T(8,128)(2,1)S(1)} %all_to_all.25.packed_ref, f32[1,256]{1,0:T(1,128)S(1)} %get-tuple-element.20.gain_ref, bf16[2560,256]{1,0:T(8,128)(2,1)S(1)} %copy-done, ...), custom_call_target="tpu_custom_call" | custom-call | tf_op jit(solution)/shard_map/convolve/pallas_call | solution.py:116
  35.1 14.1 %all_to_all.26.sums_ref = f32[16,4,128]{2,1,0:T(4,128)S(1)} all-to-all(f32[16,4,128]{2,1,0:T(4,128)S(1)} %get-tuple-element.22), channel_id=1, replica_groups=mesh['y_lo'=4,'z'=8,'x'=8,'y_hi'=2,'core'=2] {'y_lo','y_hi','core'}, dimensions={0} | all-to-all | bytes 65536 | tf_op jit(solution)/shard_map/all_to_all | solution.py:307
  49.3 19.8 %all_to_all.27.sums_ref = bf16[64,4,128]{2,1,0:T(4,128)(2,1)S(1)} all-to-all(bf16[64,4,128]{2,1,0:T(4,128)(2,1)S(1)} %merge_line.1), channel_id=1, replica_groups=mesh['y_lo'=4,'z'=8,'x'=8,'y_hi'=2,'core'=2] {'x','z'}, dimensions={0} | all-to-all | bytes 131072 | tf_op jit(solution)/shard_map/all_to_all | solution.py:307
  69.1 0.1 merge_plane.1
  69.2 11.5 %all_to_all.28.sums_ref = f32[16,4,128]{2,1,0:T(4,128)S(1)} all-to-all(f32[16,4,128]{2,1,0:T(4,128)S(1)} %merge_plane.1), channel_id=1, replica_groups=mesh['y_lo'=4,'z'=8,'x'=8,'y_hi'=2,'core'=2] {'y_lo','y_hi','core'}, dimensions={0} | all-to-all | bytes 65536 | tf_op jit(solution)/shard_map/all_to_all | solution.py:307
  80.7 1.3 %correlate.1 = bf16[32,16,128]{2,1,0:T(8,128)(2,1)S(1)} custom-call(f32[16,4,128]{2,1,0:T(4,128)S(1)} %all_to_all.28.sums_ref, bf16[32,32,128]{2,1,0:T(8,128)(2,1)S(1)} %all_to_all.25.packed_ref, bf16[32,8,128]{2,1,0:T(8,128)(2,1)S(1)} %get-tuple-element.23.conv_ref, f32[32,8,128]{2,1,0:T(8,128)S(1)} %get-tuple-element.24.gained_ref, ...), custom_call_target="tpu_custom_call" | custom-call | tf_op jit(solution)/shard_map/correlate/pallas_call | solution.py:116
  82.1 12.3 %all_to_all.29.back_ref = bf16[32,16,128]{2,1,0:T(8,128)(2,1)S(1)} all-to-all(bf16[32,16,128]{2,1,0:T(8,128)(2,1)S(1)} %correlate.1), channel_id=1, replica_groups=mesh['y_lo'=4,'z'=8,'x'=8,'y_hi'=2,'core'=2] {'y_lo','z'}, dimensions={0} | all-to-all | bytes 262144 | tf_op jit(solution)/shard_map/all_to_all | solution.py:307
  94.4 0.9 finish.1
  (1 shorter events, 0.0 us)
Async XLA Ops:
  1.7 32.0 %copy-start = (bf16[2560,256]{1,0:T(8,128)(2,1)S(1)}, bf16[2560,256]{1,0:T(8,128)(2,1)}, u32[]{:S(2)}) copy-start(bf16[2560,256]{1,0:T(8,128)(2,1)} %constant.4.clone.table_ref) | copy-start | bytes 3932164
